TPU v7x, 128 devices: a whole 4x4x4 slice. The times are simulated.
128 devices in a mesh: tok: 16 (over z, y_lo, core), feat: 8 (over y_hi, x).
Axes of the slice: x: 4, y: 4 (y_hi: 2, y_lo: 2; y = y_hi * 2 + y_lo), z: 4, core: 2. Of those that a mesh axis runs over, the one named last changes fastest.
Arguments:
- teacher: float32 [8192, 16384], P('tok', 'feat'), may hold values from -720 to 720, as said below
- student: float32 [8192, 2048], P('tok', 'feat'), may hold values from -6 to 6
- gain: float32 [16384], P('feat'), may hold values from 0.1 to 1.9
- projector: float32 [2048, 16384], P(None, 'feat'), may hold values from -0.1875 to 0.1875
- momentum: float32 [2048, 16384], P('tok', 'feat'), may hold values from -0.12 to 0.12
Outputs:
- new_projector: float32 [2048, 16384], P('tok', 'feat')
- new_momentum: float32 [2048, 16384], P('tok', 'feat')
- student_grad: float32 [8192, 2048], P('tok', 'feat')
- loss_value: float32 [], replicated
Inputs may be any that keep to these rules, and one draw needn't show every extreme that they name: `teacher`: finite real values.
All inputs are finite; a program needn't handle non-finite values.
Results may differ from a plain program's by a relative error of at most 0.00011.
Values sent between devices are 32-bit elements; how exact they have to be, the bound alone decides.
No kernel may reach another device: no remote copies, remote signals or barrier semaphores. Data moves between devices by JAX's collectives and lax.ppermute only.
A program may use at most 128 MiB of HBM per device.

v0:
```python
import jax
import jax.numpy as jnp
from jax import lax
from jax.sharding import Mesh
from jax.sharding import PartitionSpec as P

DT = 16384
TOK = ("tok_0", "tok_1", "tok_2")
FEAT = ("feat_0", "feat_1")
TOK_FEAT = ("tok_0", "tok_1", "tok_2", "feat_0", "feat_1")


norm_eps = 1e-05
momentum_rate = 0.9
step_rate = 0.5


def over_axes(value, axes):
    for axis in axes:
        value = lax.psum(value, axis)
    return value


def split_up(value, dim, devices):
    before, after = (value.shape[:dim], value.shape[dim + 1 :])
    return jnp.moveaxis(value.reshape(*before, devices, -1, *after), dim, 0)


def summed_on_arrival(value, axis, dim):
    blocks = split_up(value, dim, lax.axis_size(axis))
    arrived = lax.all_to_all(blocks, axis, split_axis=0, concat_axis=0, tiled=True)
    return arrived.sum(axis=0)


def on_device(teacher, student, gain, projector, momentum):
    highest = lax.Precision.HIGHEST
    local_rows = teacher.shape[0]
    token_count = local_rows * lax.axis_size(TOK)
    full_student = lax.all_gather(student, FEAT, axis=1, tiled=True)
    predicted = jnp.dot(
        full_student, projector, precision=highest, preferred_element_type=jnp.float32
    )
    weighted = teacher * gain[None, :]
    squares_part = jnp.sum(teacher * teacher, axis=1)
    row_total = lax.psum(squares_part, FEAT)
    row_scale = lax.rsqrt(row_total / DT + norm_eps)
    residual = predicted - weighted * row_scale[:, None]
    error_sum = over_axes(jnp.sum(residual * residual), TOK_FEAT)
    loss_value = error_sum / (token_count * DT)
    own_count = projector.shape[0] // lax.axis_size(TOK)
    proj_grad = lax.psum_scatter(
        lax.dot_general(
            full_student,
            residual,
            (((0,), (0,)), ((), ())),
            precision=highest,
            preferred_element_type=jnp.float32,
        )
        / token_count,
        TOK,
        scatter_dimension=0,
        tiled=True,
    )
    student_terms = lax.dot_general(
        residual,
        projector,
        (((1,), (1,)), ((), ())),
        precision=highest,
        preferred_element_type=jnp.float32,
    )
    student_grad = summed_on_arrival(student_terms, FEAT, 1)
    new_momentum = momentum_rate * momentum + proj_grad
    first_own = lax.axis_index(TOK) * own_count
    own_rows = lax.dynamic_slice_in_dim(projector, first_own, own_count, 0)
    new_projector = own_rows - step_rate * new_momentum
    return (new_projector, new_momentum, student_grad, loss_value)


def solution(mesh):
    split = Mesh(
        mesh.devices.reshape(4, 2, 2, 2, 4), ("tok_0", "tok_1", "tok_2", "feat_0", "feat_1")
    )
    in_specs = (P(TOK, FEAT), P(TOK, FEAT), P(FEAT), P(None, FEAT), P(TOK, FEAT))
    out_specs = (P(TOK, FEAT), P(TOK, FEAT), P(TOK, FEAT), P())
    return jax.shard_map(
        on_device, mesh=split, in_specs=in_specs, out_specs=out_specs, check_vma=False
    )
```

profile of v0, /device:TPU:0, one launch (start us, length us, event | category | flops | bytes accessed | tf_op | source)
XLA Modules:
  0.0 395.2 jit_solution(3353362954193325163)
XLA Ops:
  7.2 0.7 all-gather.2.cloned.1.call-update
  7.9 0.0 reduce-scatter.2.cloned.1.call-start
  8.0 2.5 multiply_reduce_fusion
  10.5 24.6 %psum.42 = f32[512]{0:T(512)S(1)} all-reduce(f32[512]{0:T(512)S(1)} %multiply_reduce_fusion), channel_id=1, replica_groups=mesh['tok_0'=4,'tok_1'=2,'tok_2'=2,'feat_0'=2,'feat_1'=4] {'feat_0','fea..., use_global_device_ids=true, to_apply=%region_1.0 | all-reduce | flops 512 | bytes 4096 | tf_op jit(solution)/shard_map/psum | solution.py:45
  35.1 54.8 %all-gather.2.cloned.1.call-done = f32[512,2048]{1,0:T(8,128)} async-done(((f32[512,256]{1,0:T(8,128)}), f32[512,2048]{1,0:T(8,128)}) %all-gather.2.cloned.1.call-update) | async-done | bytes 4194320 | tf_op jit(solution)/shard_map/all_gather | solution.py:39
  89.9 32.5 %fusion.6 = (f32[]{:T(128)}, f32[512,2048]{1,0:T(8,128)S(1)}) fusion(f32[512,2048]{1,0:T(8,128)} %param.5, f32[512]{0:T(512)S(1)} %add_rsqrt_fusion, f32[2048]{0:T(1024)S(1)} %copy-done.4, f32[512,2048]{1,0:T(8,128)} %all-gather.2.cloned.1.call-done, f32[2048,2048]{1,0:T(8,128)} %param.8), kind=kOutput, calls=%fused_computation.6 | convolution fusion | flops 25775046656 | bytes 29370372 | tf_op jit(solution)/shard_map/dot_general | solution.py:40
  122.4 1.9 copy-done.1
  124.3 30.1 %multiply_bitcast_fusion = f32[2048,2048]{0,1:T(8,128)} fusion(f32[512,2048]{1,0:T(8,128)S(1)} %copy-done.2, f32[512,2048]{1,0:T(8,128)S(1)} %get-tuple-element.15, f32[512,2048]{1,0:T(8,128)S(1)} %copy-done, f32[512]{0:T(512)S(1)} %add_rsqrt_fusion, f32[2048]{0:T(1024)S(1)} %copy-done.4), kind=kOutput, calls=%fused_computation | convolution fusion | flops 25777143808 | bytes 29370368 | tf_op jit(solution)/shard_map/dot_general | solution.py:52
  154.5 32.0 %fusion = f32[512,2048]{1,0:T(8,128)S(1)} fusion(f32[2048,2048]{1,0:T(8,128)} %param.8, f32[512,2048]{1,0:T(8,128)} %copy-done.1, f32[512,2048]{1,0:T(8,128)} %param.5, f32[512]{0:T(512)S(1)} %add_rsqrt_fusion, f32[2048]{0:T(1024)S(1)} %copy-done.4), kind=kOutput, calls=%fused_computation.2 | convolution fusion | flops 25772949504 | bytes 29370368 | tf_op jit(solution)/shard_map/dot_general | solution.py:64
  186.5 2.4 copy.21
  188.8 4.5 %all-to-all-start = ((f32[8,512,256]{2,1,0:T(8,128)}), f32[8,512,256]{2,1,0:T(8,128)}, u32[]{:S(2)}, u32[]{:S(2)}) async-start(f32[8,512,256]{2,1,0:T(8,128)} %bitcast.13), calls=%async_computation.1 | async-start | bytes 8388608 | tf_op jit(solution)/shard_map/all_to_all | solution.py:31
  193.4 11.3 %psum.43 = f32[]{:T(128)} all-reduce(f32[]{:T(128)} %get-tuple-element.14), channel_id=1, replica_groups=mesh['tok_0'=4,'tok_1'=2,'tok_2'=2,'feat_0'=2,'feat_1'=4] {'tok_0'}, use_global_device_ids=true, to_apply=%region_5.0 | all-reduce | flops 1 | bytes 8 | tf_op jit(solution)/shard_map/psum | solution.py:20
  204.8 47.1 %psum.44 = f32[]{:T(128)} all-reduce(f32[]{:T(128)} %psum.43), channel_id=1, replica_groups=mesh['tok_0'=4,'tok_1'=2,'tok_2'=2,'feat_0'=2,'feat_1'=4] {'tok_1'}, use_global_device_ids=true, to_apply=%region_6.0 | all-reduce | flops 1 | bytes 8 | tf_op jit(solution)/shard_map/psum | solution.py:20
  251.9 1.3 constant_dynamic-slice_fusion
  253.2 3.1 psum.45
  256.3 0.3 copy.18
  256.6 7.8 %psum.46 = f32[]{:T(128)} all-reduce(f32[]{:T(128)} %psum.45), channel_id=1, replica_groups=mesh['tok_0'=4,'tok_1'=2,'tok_2'=2,'feat_0'=2,'feat_1'=4] {'feat_0'}, use_global_device_ids=true, to_apply=%region_8.0 | all-reduce | flops 1 | bytes 8 | tf_op jit(solution)/shard_map/psum | solution.py:20
  264.4 0.3 copy.14
  264.7 9.8 %psum.47 = f32[]{:T(128)} all-reduce(f32[]{:T(128)} %psum.46), channel_id=1, replica_groups=mesh['tok_0'=4,'tok_1'=2,'tok_2'=2,'feat_0'=2,'feat_1'=4] {'feat_1'}, use_global_device_ids=true, to_apply=%region_9.0 | all-reduce | flops 1 | bytes 8 | tf_op jit(solution)/shard_map/psum | solution.py:20
  275.2 3.3 reduce_sum.28
  278.6 102.5 %reduce-scatter.2.cloned.1.call-done = f32[128,2048]{0,1:T(8,128)} async-done(((f32[2048,2048]{0,1:T(8,128)}), f32[128,2048]{0,1:T(8,128)}) %reduce-scatter.2.cloned.1.call-update) | async-done | bytes 1048592 | tf_op jit(solution)/shard_map/reduce_scatter | solution.py:51
  381.0 2.4 multiply_subtract_fusion
  383.4 2.5 copy.16
  385.9 1.3 copy.17
  (13 shorter events, 0.1 us)
Async XLA Ops:
  7.2 82.7 %copy-start.4 = (f32[2048]{0:T(1024)S(1)}, f32[2048]{0:T(1024)}, u32[]{:S(2)}) copy-start(f32[2048]{0:T(1024)} %param.7) | copy-start | bytes 24580
  7.2 82.7 %all-gather.2.cloned.1.call-start = ((), (), s32[]{:S(2)}) async-start(), calls=%async_computation.2 | async-start | bytes 4718592 | tf_op jit(solution)/shard_map/all_gather | solution.py:39
  7.9 373.1 %reduce-scatter.2.cloned.1.call-start = ((), (), s32[]{:S(2)}) async-start(), calls=%async_computation.3 | async-start | bytes 17825792 | tf_op jit(solution)/shard_map/reduce_scatter | solution.py:51
  89.9 34.5 %copy-start = (f32[512,2048]{1,0:T(8,128)S(1)}, f32[512,2048]{1,0:T(8,128)}, u32[]{:S(2)}) copy-start(f32[512,2048]{1,0:T(8,128)} %param.5) | copy-start | bytes 12582916
  89.9 34.5 %copy-start.2 = (f32[512,2048]{1,0:T(8,128)S(1)}, f32[512,2048]{1,0:T(8,128)}, u32[]{:S(2)}) copy-start(f32[512,2048]{1,0:T(8,128)} %all-gather.2.cloned.1.call-done) | copy-start | bytes 12582916
  122.4 1.9 copy-start.1
  188.8 86.4 %all-to-all-start = ((f32[8,512,256]{2,1,0:T(8,128)}), f32[8,512,256]{2,1,0:T(8,128)}, u32[]{:S(2)}, u32[]{:S(2)}) async-start(f32[8,512,256]{2,1,0:T(8,128)} %bitcast.13), calls=%async_computation.1 | async-start | bytes 8388608 | tf_op jit(solution)/shard_map/all_to_all | solution.py:31
  193.4 71.0 %copy-start.3 = (f32[128,2048]{1,0:T(8,128)S(1)}, f32[128,2048]{1,0:T(8,128)}, u32[]{:S(2)}) copy-start(f32[128,2048]{1,0:T(8,128)} %param.9) | copy-start | bytes 3145732
Sparse Core Ops, SparseCore 0:
  10.2 79.6 all-gather.1
  154.6 226.3 reduce-scatter.1
where the time goes:
time: 396 us; the launch traced here: 395 us
  waiting for transfers between devices  158 us (40%)
  blocking collectives  104 us (26%)
  matrix products  94.6 us (24%)
  between operations  15.9 us (4%)
  local copies, waits for them, and re-layouts  10.1 us (3%)
  other arithmetic  8.28 us (2%)
  starting transfers between devices  4.62 us (1%)
    reduce_scatter x1, waiting for transfers between devices, on_device(): lax.psum_scatter(lax.dot_general(full_student, residual, (((0,), (0,)), (...  102 us
    psum x5, blocking collectives, over_axes(): value = lax.psum(value, axis)  79.2 us
    all_gather x1, waiting for transfers between devices, on_device(): full_student = lax.all_gather(student, FEAT, axis=1, tiled=True)  54.8 us
    dot_general x1, matrix products, on_device(): jnp.dot(full_student, projector, precision=highest, preferred_element_typ...  32.5 us
    dot_general x1, matrix products, on_device(): lax.dot_general(residual, projector, (((1,), (1,)), ((), ())), precision=...  32 us
    dot_general x1, matrix products, on_device(): lax.dot_general(full_student, residual, (((0,), (0,)), ((), ())), precisi...  30.1 us
    psum x1, blocking collectives, on_device(): row_total = lax.psum(squares_part, FEAT)  24.6 us
  transfers between devices with their start and end apart: 3, of which 2 were waited for; matrix products, arithmetic and copies ran while one was open for 11% of the time, Pallas kernels for 0%

commit v1 on v0

v1 whole, which is shorter than its diff:
```python
import functools

import jax
import jax.numpy as jnp
from jax import lax
from jax.experimental import pallas as pl
from jax.experimental.pallas import tpu as pltpu
from jax.sharding import Mesh
from jax.sharding import PartitionSpec as P

DT = 16384
TOKENS = 8192
TOK = ("tok_0", "tok_1", "tok_2")
FEAT = ("feat_0", "feat_1")
Z, YLO, CORE, YHI, X = "tok_0", "tok_1", "tok_2", "feat_0", "feat_1"

norm_eps = 1e-05
momentum_rate = 0.9
step_rate = 0.5


F32, BF16 = jnp.float32, jnp.bfloat16
CY = 768
TN = 256
MIB = 1 << 20


def cost(flops, moved):
    return pl.CostEstimate(flops=flops, bytes_accessed=moved, transcendentals=0)


def halves(value):
    hi = value.astype(BF16)
    return hi, (value - hi.astype(F32)).astype(BF16)


def lhs3(hi, lo):
    return jnp.concatenate([hi, lo, hi], 1)


def rhs3(hi, lo, axis):
    return jnp.concatenate([hi, hi, lo], axis)


def dot(a, b, dims):
    return lax.dot_general(a, b, (dims, ((), ())), preferred_element_type=F32)


def shift(value, axis, by, size):
    return lax.ppermute(value, axis, [(i, (i + by) % size) for i in range(size)])


def sum_pair(value, axis, far=False):
    size = lax.axis_size(axis)
    step = 2 if far else 1
    return value + lax.ppermute(value, axis, [(i, i ^ step) for i in range(size)])


def after(index, *earlier):
    return lax.optimization_barrier((index, *earlier))[0]


def kernel(body, index, args, **spec):
    shapes = spec.pop("out_shape")
    grid_spec = pltpu.PrefetchScalarGridSpec(num_scalar_prefetch=1, **spec.pop("grid"))
    return pl.pallas_call(
        body,
        grid_spec=grid_spec,
        out_shape=shapes,
        compiler_params=pltpu.CompilerParams(vmem_limit_bytes=spec.pop("vmem") * MIB),
        **spec,
    )(index, *args)


FEATURE = {(dy, dx): dy * 4 + dx for dy in (0, 1) for dx in range(4)}
SLOT = {(dz, dy): 8 + dz * 2 + dy for dz in range(4) for dy in (0, 1)}
CORE_AT = 16


def table():
    z, ylo, core = lax.axis_index(Z), lax.axis_index(YLO), lax.axis_index(CORE)
    yhi, x = lax.axis_index(YHI), lax.axis_index(X)
    entries = [(yhi ^ dy) * 4 + (x + dx) % 4 for dy, dx in FEATURE]
    for dz, dy in SLOT:
        index = ((z + dz) % 4) * 2 + (ylo ^ dy)
        entries.append(((index // 4) ^ yhi) * 4 + (index % 4 - x) % 4)
    entries.append(core)
    return jnp.stack(entries).astype(jnp.int32)


EXTRA = 8


def pack_body(index, teacher, student, out, total):
    part = teacher[...]

    @pl.when(pl.program_id(0) == 0)
    def _():
        total[...] = jnp.zeros_like(total)

    squares = part * part
    folded = squares[:, :128]
    for k in range(1, part.shape[1] // 128):
        folded = folded + squares[:, k * 128 : (k + 1) * 128]
    total[...] += folded

    @pl.when(pl.program_id(0) == pl.num_programs(0) - 1)
    def _():
        half = student.shape[0] // 2
        sums = jnp.sum(total[...].T, axis=0, keepdims=True)
        for h in (0, 1):
            out[h, :half, :] = student[h * half : (h + 1) * half, :]
            out[h, half:, :] = jnp.broadcast_to(sums[:, h * half : (h + 1) * half], (EXTRA, half))


def packed(index, teacher, student):
    rows, cols = teacher.shape
    width = student.shape[1]
    shape = (2, rows // 2 + EXTRA, width)
    return kernel(
        pack_body,
        index,
        [teacher, student],
        grid=dict(
            grid=(4,),
            in_specs=[
                pl.BlockSpec((rows, cols // 4), lambda j, idx: (0, j)),
                pl.BlockSpec((rows, width), lambda j, idx: (0, 0)),
            ],
            out_specs=pl.BlockSpec(shape, lambda j, idx: (0, 0, 0)),
            scratch_shapes=[pltpu.VMEM((rows, 128), F32)],
        ),
        out_shape=jax.ShapeDtypeStruct(shape, F32),
        cost_estimate=cost(0, 4 * rows * cols),
        vmem=16,
    )


def forward_body(count, tile, with_acc, sums, *refs):
    refs = list(refs)
    refs.pop(0)
    blocks = [refs.pop(0) for _ in range(count)]
    parts = [refs.pop(0) for _ in range(count)]
    left, right = [], []
    half = blocks[0].shape[1] - EXTRA
    for k in range(count):
        block = jnp.concatenate([blocks[k][0, :half, :], blocks[k][1, :half, :]], 0)
        left.append(lhs3(*halves(block)))
        right.append(rhs3(*halves(parts[k][...]), 0))
    total = dot(jnp.concatenate(left, 1), jnp.concatenate(right, 0), ((1,), (0,)))
    if with_acc:
        total = total + refs.pop(0)[...]
    if not sums:
        refs[0][...] = total
        return
    partial = [refs.pop(0)[...] for _ in range(sums)]
    while len(partial) > 1:
        partial = [p + q for p, q in zip(partial[::2], partial[1::2])]
    teacher, gain, out, error = refs
    scale = lax.rsqrt(partial[0] / DT + norm_eps)
    scale = jnp.concatenate([scale[0].T, scale[1].T], 0)[:, :1]
    residual = total - (teacher[...] * scale) * gain[...]
    out[...] = residual

    @pl.when(pl.program_id(0) == 0)
    def _():
        error[...] = jnp.zeros_like(error)

    error[...] += jnp.sum((residual * residual).reshape(-1, 8, tile), axis=0)


def forward(index, pieces, at, projector, acc=None, final=None, first=0, tiles=4, tile=512):
    count = len(pieces)
    width = pieces[0].shape[2]
    half = pieces[0].shape[1] - EXTRA
    rows = 2 * half
    in_specs = [pl.BlockSpec(p.shape, lambda j, idx: (0, 0, 0)) for p in pieces]
    args = list(pieces)
    for k in range(count):
        args.append(projector)
        in_specs.append(
            pl.BlockSpec(
                (width, tile), functools.partial(lambda a, j, idx: (idx[a], j + first), at[k])
            )
        )
    if acc is not None:
        args.append(acc)
        in_specs.append(pl.BlockSpec((rows, tile), lambda j, idx: (0, j + first)))
    out_shape = jax.ShapeDtypeStruct((rows, tile * tiles), F32)
    out_specs = pl.BlockSpec((rows, tile), lambda j, idx: (0, j))
    sums = 0
    if final is not None:
        every, teacher, gain = final
        sums = len(every)
        args += [*every, teacher, gain]
        in_specs += [pl.BlockSpec((2, EXTRA, width), lambda j, idx: (0, half // EXTRA, 0))] * sums
        in_specs += [
            pl.BlockSpec((rows, tile), lambda j, idx: (0, j + first)),
            pl.BlockSpec((1, tile), lambda j, idx: (0, j + first)),
        ]
        out_shape = (out_shape, jax.ShapeDtypeStruct((8, tile), F32))
        out_specs = (out_specs, pl.BlockSpec((8, tile), lambda j, idx: (0, 0)))
    return kernel(
        functools.partial(forward_body, count, tile, acc is not None, sums),
        index,
        args,
        grid=dict(grid=(tiles,), in_specs=in_specs, out_specs=out_specs),
        out_shape=out_shape,
        cost_estimate=cost(6 * rows * width * count * tile * tiles, 8 * rows * tile * tiles),
        vmem=40,
    )


def prepare_body(count, slots, kept, *refs):
    refs = list(refs)
    refs.pop(0)
    own = [refs.pop(0) for _ in range(count)]
    other = [refs.pop(0) for _ in range(count)]
    if kept:
        old_hi, old_lo = refs.pop(0), refs.pop(0)
    hi, lo, sent = refs
    half = own[0].shape[1] - EXTRA
    if kept:
        for k in kept:
            hi[k] = old_hi[k]
            lo[k] = old_lo[k]
    for k in range(count):
        for h in (0, 1):
            rows = pl.ds(h * half, half)
            a, b = halves(own[k][h, :half, :].T)
            hi[slots[k], :, rows] = a
            lo[slots[k], :, rows] = b
            sent[k, rows, :] = other[k][h, :half, :]


def prepare(index, pieces, slots, old=None):
    count = len(pieces)
    _, long, width = pieces[0].shape
    rows = 2 * (long - EXTRA)
    in_specs = [
        pl.BlockSpec(
            (2, long, width // 2),
            functools.partial(lambda o, j, idx: (0, 0, idx[CORE_AT] ^ o), other),
        )
        for other in (0, 1)
        for _ in pieces
    ]
    args = [*pieces, *pieces]
    split = jax.ShapeDtypeStruct((8, width // 2, rows), BF16)
    sent = jax.ShapeDtypeStruct((count, rows, width // 2), F32)
    whole = [pl.BlockSpec(s.shape, lambda j, idx: (0, 0, 0)) for s in (split, split, sent)]
    kept = ()
    if old is not None:
        args += list(old)
        in_specs += whole[:2]
        kept = tuple(k for k in range(8) if k not in slots)
    return kernel(
        functools.partial(prepare_body, count, slots, kept),
        index,
        args,
        grid=dict(grid=(1,), in_specs=in_specs, out_specs=whole),
        out_shape=(split, split, sent),
        cost_estimate=cost(0, 8 * MIB),
        vmem=16,
    )


def turn_body(slots, index, first, second, hi, lo):
    for part, where in zip((first, second), slots):
        for k, slot in enumerate(where):
            a, b = halves(part[k].T)
            hi[slot], lo[slot] = a, b


def turned(index, came, slots):
    _, rows, width = came[0].shape
    split = jax.ShapeDtypeStruct((8, width, rows), BF16)
    spec = pl.BlockSpec((8, width, rows), lambda j, idx: (0, 0, 0))
    return kernel(
        functools.partial(turn_body, slots),
        index,
        came,
        grid=dict(
            grid=(1,),
            in_specs=[pl.BlockSpec(c.shape, lambda j, idx: (0, 0, 0)) for c in came],
            out_specs=(spec, spec),
        ),
        out_shape=(split, split),
        cost_estimate=cost(0, 4 * MIB),
        vmem=16,
    )


def grad_body(count, stacked, *refs):
    refs = list(refs)
    refs.pop(0)
    blocks = [[refs.pop(0)[0] for _ in range(count)] for _ in range(4)]
    mine, other = refs.pop(0)[...], refs.pop(0)[...]
    parts = [jnp.concatenate(part, 0) for part in blocks]
    left = jnp.concatenate([lhs3(*parts[:2]), lhs3(*parts[2:])], 1)
    right = jnp.concatenate([rhs3(*halves(mine), 0), rhs3(*halves(other), 0)], 0)
    total = dot(left, right, ((1,), (0,)))
    rows = total.shape[0] // count
    for k in range(count):
        if stacked:
            refs[0][k] = total[k * rows : (k + 1) * rows]
        else:
            refs[k][...] = total[k * rows : (k + 1) * rows]


def grad_blocks(index, at, splits, mine, other, stacked=False):
    count = len(at)
    _, rows, tokens = splits[0].shape
    cols = mine.shape[1]
    in_specs, args = [], []
    for part in splits:
        for k in range(count):
            args.append(part)
            in_specs.append(
                pl.BlockSpec(
                    (1, rows, tokens), functools.partial(lambda a, j, idx: (idx[a], 0, 0), at[k])
                )
            )
    in_specs += [pl.BlockSpec((tokens, TN), lambda j, idx: (0, j))] * 2
    if stacked:
        out = jax.ShapeDtypeStruct((count, rows, cols), F32)
        out_specs = pl.BlockSpec((count, rows, TN), lambda j, idx: (0, 0, j))
    else:
        out = [jax.ShapeDtypeStruct((rows, cols), F32)] * count
        out_specs = [pl.BlockSpec((rows, TN), lambda j, idx: (0, j))] * count
    return kernel(
        functools.partial(grad_body, count, stacked),
        index,
        [*args, mine, other],
        grid=dict(grid=(cols // TN,), in_specs=in_specs, out_specs=out_specs),
        out_shape=out,
        cost_estimate=cost(12 * rows * count * tokens * cols, 8 * tokens * cols),
        vmem=24,
    )


def state_body(count, split_at, index, part, res_y, res_z, *refs):
    outs, (hi, lo) = refs[:count], refs[count:]

    @pl.when(pl.program_id(0) == 0)
    def _():
        hi[:, :split_at], lo[:, :split_at] = halves(res_y[...])
        hi[:, split_at:], lo[:, split_at:] = halves(res_z[...])

    dims = ((1,), (1,))
    whi, wlo = halves(part[...])
    value = dot(hi[...], whi, dims) + (dot(lo[...], whi, dims) + dot(hi[...], wlo, dims))
    for k in range(count):

        @pl.when(pl.program_id(0) == k)
        def _(k=k):
            outs[k][...] = value


def state_blocks(index, at, projector, res_y, res_z):
    count = len(at)
    rows, split_at = res_y.shape
    cols, width = projector.shape[1], 256

    def which(j, idx):
        row = idx[at[0]]
        for k in range(1, count):
            row = jnp.where(j == k, idx[at[k]], row)
        return (row, 0)

    return kernel(
        functools.partial(state_body, count, split_at),
        index,
        [projector, res_y, res_z],
        grid=dict(
            grid=(count,),
            in_specs=[
                pl.BlockSpec((width, cols), which),
                pl.BlockSpec(res_y.shape, lambda j, idx: (0, 0)),
                pl.BlockSpec(res_z.shape, lambda j, idx: (0, 0)),
            ],
            out_specs=[pl.BlockSpec((rows, width), lambda j, idx: (0, 0))] * count,
            scratch_shapes=[pltpu.VMEM((rows, cols), BF16)] * 2,
        ),
        out_shape=[jax.ShapeDtypeStruct((rows, width), F32)] * count,
        cost_estimate=cost(6 * rows * count * width * cols, 8 * MIB),
        vmem=40,
    )


def in_layer(teacher, student, gain, projector, momentum):
    _, cols = teacher.shape
    width = student.shape[1]
    half = width // 2
    index = table()

    def at(*pairs):
        return [FEATURE[p] for p in pairs]

    own = packed(index, teacher, student)
    upper = shift(own, YHI, 1, 2)
    left, right = shift(own, X, 1, 4), shift(own, X, -1, 4)
    far = shift(own, X, 2, 4)
    acc = forward(index, [own], at((0, 0)), projector)
    acc = forward(after(index, acc), [upper], at((1, 0)), projector, acc)
    ul, ur = shift(upper, X, 1, 4), shift(upper, X, -1, 4)
    ufar = shift(far, YHI, 1, 2)
    acc = forward(after(index, acc), [left, right, far], at((0, 3), (0, 1), (0, 2)), projector, acc)
    hi, lo, sent_a = prepare(after(index, acc), [own, right, far, left], (0, 1, 2, 3))
    came_a = shift(sent_a, CORE, 1, 2)
    every = [own, far, left, right, upper, ufar, ul, ur]
    args = ([ul, ur, ufar], at((1, 3), (1, 1), (1, 2)), projector, acc)
    args += ((every, teacher, gain.reshape(1, cols)),)
    res_y, err_y = forward(after(index, sent_a), *args, 0, CY // TN, TN)
    other_y = shift(res_y, CORE, 1, 2)
    res_z, err_z = forward(after(index, res_y), *args, CY // TN, (cols - CY) // TN, TN)
    other_z = shift(res_z, CORE, 1, 2)
    error = jnp.sum(err_y + err_z).reshape(1)
    error = sum_pair(error, YHI)
    hi, lo, sent_b = prepare(after(index, res_z), [upper, ur, ufar, ul], (4, 5, 6, 7), (hi, lo))
    came_b = shift(sent_b, CORE, 1, 2)
    error = sum_pair(error, YLO)

    def state(index, *pairs):
        return state_blocks(index, at(*pairs), projector, res_y, res_z)

    sfar = state(after(index, sent_b), (0, 2), (1, 2))
    sfo, sft = shift(sfar[0], X, 1, 4), shift(sfar[1], X, -1, 4)
    splits = (
        hi,
        lo,
        *turned(after(index, sfar[0]), (came_a, came_b), ((0, 1, 2, 3), (4, 5, 6, 7))),
    )

    def grad_y(index, *pairs, stacked=False):
        return grad_blocks(index, [SLOT[p] for p in pairs], splits, res_y, other_y, stacked)

    def grad_z(index, *pairs):
        return grad_blocks(index, [SLOT[p] for p in pairs], splits, res_z, other_z)

    far_own, far_oth = grad_z(index, (2, 0), (2, 1))
    far_own_came, far_oth_came = shift(far_own, Z, 1, 4), shift(far_oth, Z, -1, 4)
    ys = grad_y(after(index, far_own, error), (2, 1), (1, 1), (3, 1), (0, 1), stacked=True)
    ys_came = shift(ys, YLO, 1, 2)
    error = sum_pair(error, CORE)
    up_own, up_oth, down_own, down_oth = grad_z(after(index, ys), (1, 0), (1, 1), (3, 0), (3, 1))
    s1o, s1t, s3o, s3t = state(after(index, up_own), (0, 1), (1, 1), (0, 3), (1, 3))
    up = shift(jnp.stack([up_own + far_own_came, up_oth]), Z, 1, 4)
    down = shift(jnp.stack([down_own, down_oth + far_oth_came]), Z, -1, 4)
    sup = shift(jnp.stack([s1o + sfo, s1t]), X, 1, 4)
    sdown = shift(jnp.stack([s3o, s3t + sft]), X, -1, 4)
    two, one, three, zero = grad_y(after(index, s1o), (2, 0), (1, 0), (3, 0), (0, 0))
    cut = half // 2
    two = two + ys_came[0]
    one, three = one + ys_came[1], three + ys_came[2]
    zero_own, zero_oth = grad_z(after(index, zero), (0, 0), (0, 1))
    s0o, s0t = state(after(index, zero_own), (0, 0), (1, 0))
    two, _ = lax.optimization_barrier((two, s0o))
    yfo, yft = shift(two[:cut], Z, 1, 4), shift(two[cut:], Z, -1, 4)
    z_came = shift(zero_oth + (up[1] + down[1]), YLO, 1, 2)
    yup = shift(jnp.concatenate([one[:cut] + yfo, one[cut:]], 0), Z, 1, 4)
    ydown = shift(jnp.concatenate([three[:cut], three[cut:] + yft], 0), Z, -1, 4)
    error = sum_pair(after(error, sup, sdown), X)
    error = sum_pair(error, X, far=True)
    s_came = shift(s0t + (sup[1] + sdown[1]), YHI, 1, 2)
    error = sum_pair(after(error, yup, ydown), Z)
    error = sum_pair(error, Z, far=True)
    grad_hi = (zero_own + (up[0] + down[0])) + z_came
    grad_lo = (zero + ys_came[3]) + (yup + ydown)
    proj_grad = jnp.concatenate([grad_lo, grad_hi], 1) / TOKENS
    student_grad = (s0o + (sup[0] + sdown[0])) + s_came
    loss_value = error[0] / (TOKENS * DT)

    new_momentum = momentum_rate * momentum + proj_grad
    own_block = lax.axis_index(Z) * 4 + lax.axis_index(YLO) * 2 + lax.axis_index(CORE)
    own_rows = lax.dynamic_slice_in_dim(projector, own_block * half, half, 0)
    new_projector = own_rows - step_rate * new_momentum
    return (new_projector, new_momentum, student_grad, loss_value)


def solution(mesh):
    split = Mesh(
        mesh.devices.reshape(4, 2, 2, 2, 4), ("tok_0", "tok_1", "tok_2", "feat_0", "feat_1")
    )
    in_specs = (P(TOK, FEAT), P(TOK, FEAT), P(FEAT), P(None, FEAT), P(TOK, FEAT))
    out_specs = (P(TOK, FEAT), P(TOK, FEAT), P(TOK, FEAT), P())
    return jax.shard_map(
        in_layer, mesh=split, in_specs=in_specs, out_specs=out_specs, check_vma=False
    )
```

time: 396 us -> 208 us (0.53)
  waiting for transfers between devices: 158 us -> 42.2 us
  blocking collectives: 104 us -> 0 us
  matrix products: 94.6 us -> 0 us
  Pallas kernels: 0 us -> 81.5 us
  starting transfers between devices: 4.62 us -> 49.7 us
  other arithmetic: 8.28 us -> 18.5 us
  between operations: 15.9 us -> 7.58 us
    psum x6 -> x0, blocking collectives: 104 us -> none  [the longest x5 79.2 us: over_axes(): value = lax.psum(value, axis)]
    reduce_scatter x1 -> x0, waiting for transfers between devices: 102 us -> none  [on_device(): lax.psum_scatter(lax.dot_general(full_student, residual, (((0,), (0,)), (...]
    dot_general x3 -> x0, matrix products: 94.6 us -> none  [the longest x1 32.5 us: on_device(): jnp.dot(full_student, projector, precision=highest, preferred_element_typ...]
    pallas_call x0 -> x17, Pallas kernels: none -> 81.5 us  [kernel(): pl.pallas_call(body, grid_spec=grid_spec, out_shape=shapes, compiler_para...]
    all_gather x1 -> x0, waiting for transfers between devices: 54.8 us -> none  [on_device(): full_student = lax.all_gather(student, FEAT, axis=1, tiled=True)]
    ppermute x0 -> x33, starting transfers between devices: none -> 49.7 us  [the longest x26 36.4 us: shift(): lax.ppermute(value, axis, [(i, (i + by) % size) for i in range(size)])]
    ppermute x0 -> x33, waiting for transfers between devices: none -> 42.2 us  [the longest x26 33.4 us: shift(): lax.ppermute(value, axis, [(i, (i + by) % size) for i in range(size)])]
    add x0 -> x7, other arithmetic: none -> 8.57 us  [the longest x1 2.39 us: in_layer(): student_grad = s0o + (sup[0] + sdown[0]) + s_came]
  transfers between devices with their start and end apart: 3 -> 33, of which waited for: 2 -> 14; matrix products, arithmetic and copies ran while one was open for 11% -> 7% of each run, Pallas kernels for 0% -> 33%
where the time goes in v1:
time: 208 us; the launch traced here: 207 us
  Pallas kernels  81.5 us (39%)
  starting transfers between devices  49.7 us (24%)
  waiting for transfers between devices  42.2 us (20%)
  other arithmetic  18.5 us (9%)
  local copies, waits for them, and re-layouts  7.8 us (4%)
  between operations  7.58 us (4%)
    pallas_call x17, Pallas kernels, kernel(): pl.pallas_call(body, grid_spec=grid_spec, out_shape=shapes, compiler_para...  81.5 us
    ppermute x26, starting transfers between devices, shift(): lax.ppermute(value, axis, [(i, (i + by) % size) for i in range(size)])  36.4 us
    ppermute x26, waiting for transfers between devices, shift(): lax.ppermute(value, axis, [(i, (i + by) % size) for i in range(size)])  33.4 us
    ppermute x7, starting transfers between devices, sum_pair(): lax.ppermute(value, axis, [(i, i ^ step) for i in range(size)])  13.3 us
    ppermute x7, waiting for transfers between devices, sum_pair(): lax.ppermute(value, axis, [(i, i ^ step) for i in range(size)])  8.78 us
    unnamed x38, local copies, waits for them, and re-layouts  7.67 us
  transfers between devices with their start and end apart: 33, of which 14 were waited for; matrix products, arithmetic and copies ran while one was open for 7% of the time, Pallas kernels for 33%

profile of v1, /device:TPU:0, one launch (start us, length us, event | category | flops | bytes accessed | tf_op | source)
XLA Modules:
  0.0 207.3 jit_solution(13616900104991225184)
XLA Ops:
  6.1 3.4 %collective-permute-start = (f32[2,264,256]{2,1,0:T(8,128)S(1)}, f32[2,264,256]{2,1,0:T(8,128)S(1)}, u32[]{:S(2)}, u32[]{:S(2)}) collective-permute-start(f32[2,264,256]{2,1,0:T(8,128)S(1)} %shard_map.84.refs_1_.refs_5_.refs_8_), channel_id=1, source_target_pairs={{0,4},{4,0},{1,5},{5,1},{2,6},{6,2},{3,7},{7,3},{8,12},{12,8},{9,1... | collective-permute-start | bytes 1622024 | tf_op jit(solution)/shard_map/ppermute | solution.py:50
  9.5 3.0 %collective-permute-start.3 = (f32[2,264,256]{2,1,0:T(8,128)S(1)}, f32[2,264,256]{2,1,0:T(8,128)S(1)}, u32[]{:S(2)}, u32[]{:S(2)}) collective-permute-start(f32[2,264,256]{2,1,0:T(8,128)S(1)} %shard_map.84.refs_1_.refs_5_.refs_8_), channel_id=1, source_target_pairs={{0,2},{1,3},{2,0},{3,1},{4,6},{5,7},{6,4},{7,5},{8,10},{9,11},{10,... | collective-permute-start | bytes 1622024 | tf_op jit(solution)/shard_map/ppermute | solution.py:50
  14.5 4.6 %shard_map.85.refs_3_ = f32[512,2048]{1,0:T(8,128)S(1)} custom-call(s32[17]{0:T(128)S(1)} %stack.107.index.refs_0_, f32[2,264,256]{2,1,0:T(8,128)S(1)} %shard_map.84.refs_1_.refs_5_.refs_8_, f32[2048,2048]{1,0:T(8,128)} %part.5), custom_call_target="tpu_custom_call" | custom-call | flops 1610612736 | bytes 8388608 | tf_op jit(solution)/shard_map/pallas_call | solution.py:66
  27.8 4.7 %shard_map.86.refs_7_ = f32[512,2048]{1,0:T(8,128)S(1)} custom-call(s32[17]{0:T(128)S(1)} %stack.107.index.refs_0_, f32[2,264,256]{2,1,0:T(8,128)S(1)} %collective-permute-done.refs_1_.refs_12_.refs_5_, f32[2048,2048]{1,0:T(8,128)} %part.5, f32[512,2048]{1,0:T(8,128)S(1)} %shard_map.85.refs_3_), custom_call_target="tpu_custom_call" | custom-call | flops 1610612736 | bytes 8388608 | tf_op jit(solution)/shard_map/pallas_call | solution.py:66
  32.6 5.3 %collective-permute-done.2.refs_2_.refs_6_.refs_11_ = f32[2,264,256]{2,1,0:T(8,128)S(1)} collective-permute-done((f32[2,264,256]{2,1,0:T(8,128)S(1)}, f32[2,264,256]{2,1,0:T(8,128)S(1)}, u32[]{:S(2)}, u32[]{:S(2)}) %collective-permute-start.2) | collective-permute-done | bytes 540704 | tf_op jit(solution)/shard_map/ppermute | solution.py:50
  37.8 8.1 %shard_map.87.refs_7_ = f32[512,2048]{1,0:T(8,128)S(1)} custom-call(s32[17]{0:T(128)S(1)} %stack.107.index.refs_0_, f32[2,264,256]{2,1,0:T(8,128)S(1)} %collective-permute-done.1.refs_1_.refs_4_.refs_8_.refs_10_, f32[2,264,256]{2,1,0:T(8,128)S(1)} %collective-permute-done.2.refs_2_.refs_6_.refs_11_, ...), custom_call_target="tpu_custom_call" | custom-call | flops 4831838208 | bytes 8388608 | tf_op jit(solution)/shard_map/pallas_call | solution.py:66
  48.6 4.7 %shard_map.89 = (f32[512,768]{1,0:T(8,128)S(1)}, f32[8,256]{1,0:T(8,128)S(1)}) custom-call(s32[17]{0:T(128)S(1)} %stack.107.index.refs_0_, f32[2,264,256]{2,1,0:T(8,128)S(1)} %collective-permute-done.4.refs_1_.refs_14_.refs_4_.refs_8_, f32[2,264,256]{2,1,0:T(8,128)S(1)} %collective-permute-done.5.refs_2_.refs_15_.refs_6_, ...), custom_call_target="tpu_custom_call" | custom-call | flops 1811939328 | bytes 3145728 | tf_op jit(solution)/shard_map/pallas_call | solution.py:66
  56.5 7.4 %shard_map.90 = (f32[512,1280]{1,0:T(8,128)S(1)}, f32[8,256]{1,0:T(8,128)S(1)}) custom-call(s32[17]{0:T(128)S(1)} %stack.107.index.refs_0_, f32[2,264,256]{2,1,0:T(8,128)S(1)} %collective-permute-done.4.refs_1_.refs_14_.refs_4_.refs_8_, f32[2,264,256]{2,1,0:T(8,128)S(1)} %collective-permute-done.5.refs_2_.refs_15_.refs_6_, ...), custom_call_target="tpu_custom_call" | custom-call | flops 3019898880 | bytes 5242880 | tf_op jit(solution)/shard_map/pallas_call | solution.py:66
  66.9 6.6 %shard_map.92 = (f32[512,256]{1,0:T(8,128)S(1)}, f32[512,256]{1,0:T(8,128)S(1)}) custom-call(s32[17]{0:T(128)S(1)} %stack.107.index.refs_0_, f32[2048,2048]{1,0:T(8,128)} %part.5, f32[512,768]{1,0:T(8,128)S(1)} %get-tuple-element.58.res_y.refs_17_, f32[512,1280]{1,0:T(8,128)S(1)} %get-tuple-element.60.res_z.refs_9_.refs_17_), custom_call_target="tpu_custom_call" | custom-call | flops 3221225472 | bytes 8388608 | tf_op jit(solution)/shard_map/pallas_call | solution.py:66
  74.8 3.1 %collective-permute-start.11 = (f32[1]{0:T(128)}, f32[1]{0:T(128)}, u32[]{:S(2)}, u32[]{:S(2)}) collective-permute-start(f32[1]{0:T(128)} %add.357), channel_id=1, source_target_pairs={{0,16},{16,0},{1,17},{17,1},{2,18},{18,2},{3,19},{19,3},{4,20},{20... | collective-permute-start | bytes 20 | tf_op jit(solution)/shard_map/ppermute | solution.py:56
  83.9 4.2 %shard_map.94 = (f32[128,1280]{1,0:T(8,128)S(1)}, f32[128,1280]{1,0:T(8,128)S(1)}) custom-call(s32[17]{0:T(128)S(1)} %stack.107.index.refs_0_, bf16[8,128,512]{2,1,0:T(8,128)(2,1)S(1)} %get-tuple-element.64.refs_1_.refs_2_.refs_3_.refs_4_, bf16[8,128,512]{2,1,0:T(8,128)(2,1)S(1)} %get-tuple-element.64.refs_1_.refs_2_.refs_3_.refs_4_, ...), custom_call_target="tpu_custom_call" | custom-call | flops 2013265920 | bytes 5242880 | tf_op jit(solution)/shard_map/pallas_call | solution.py:66
  90.1 4.0 %shard_map.95 = f32[4,128,768]{2,1,0:T(8,128)S(1)} custom-call(s32[17]{0:T(128)S(1)} %stack.107.index.refs_0_, bf16[8,128,512]{2,1,0:T(8,128)(2,1)S(1)} %get-tuple-element.64.refs_1_.refs_2_.refs_3_.refs_4_, bf16[8,128,512]{2,1,0:T(8,128)(2,1)S(1)} %get-tuple-element.64.refs_1_.refs_2_.refs_3_.refs_4_, ...), custom_call_target="tpu_custom_call" | custom-call | flops 2415919104 | bytes 3145728 | tf_op jit(solution)/shard_map/pallas_call | solution.py:66
  97.9 6.4 %shard_map.96 = (f32[128,1280]{1,0:T(8,128)S(1)}, f32[128,1280]{1,0:T(8,128)S(1)}, f32[128,1280]{1,0:T(8,128)S(1)}, f32[128,1280]{1,0:T(8,128)S(1)}) custom-call(s32[17]{0:T(128)S(1)} %stack.107.index.refs_0_, bf16[8,128,512]{2,1,0:T(8,128)(2,1)S(1)} %get-tuple-element.64.refs_1_.refs_2_.refs_3_.refs_4_, ...), custom_call_target="tpu_custom_call" | custom-call | flops 4026531840 | bytes 5242880 | tf_op jit(solution)/shard_map/pallas_call | solution.py:66
  104.2 10.4 %shard_map.97 = (f32[512,256]{1,0:T(8,128)S(1)}, f32[512,256]{1,0:T(8,128)S(1)}, f32[512,256]{1,0:T(8,128)S(1)}, f32[512,256]{1,0:T(8,128)S(1)}) custom-call(s32[17]{0:T(128)S(1)} %stack.107.index.refs_0_, f32[2048,2048]{1,0:T(8,128)} %part.5, f32[512,768]{1,0:T(8,128)S(1)} %get-tuple-element.58.res_y.refs_17_, ...), custom_call_target="tpu_custom_call" | custom-call | flops 6442450944 | bytes 8388608 | tf_op jit(solution)/shard_map/pallas_call | solution.py:66
  114.6 4.1 %shard_map.98 = (f32[128,768]{1,0:T(8,128)S(1)}, f32[128,768]{1,0:T(8,128)S(1)}, f32[128,768]{1,0:T(8,128)S(1)}, f32[128,768]{1,0:T(8,128)S(1)}) custom-call(s32[17]{0:T(128)S(1)} %stack.107.index.refs_0_, bf16[8,128,512]{2,1,0:T(8,128)(2,1)S(1)} %get-tuple-element.64.refs_1_.refs_2_.refs_3_.refs_4_, ...), custom_call_target="tpu_custom_call" | custom-call | flops 2415919104 | bytes 3145728 | tf_op jit(solution)/shard_map/pallas_call | solution.py:66
  118.7 4.2 %shard_map.99 = (f32[128,1280]{1,0:T(8,128)S(1)}, f32[128,1280]{1,0:T(8,128)S(1)}) custom-call(s32[17]{0:T(128)S(1)} %stack.107.index.refs_0_, bf16[8,128,512]{2,1,0:T(8,128)(2,1)S(1)} %get-tuple-element.64.refs_1_.refs_2_.refs_3_.refs_4_, bf16[8,128,512]{2,1,0:T(8,128)(2,1)S(1)} %get-tuple-element.64.refs_1_.refs_2_.refs_3_.refs_4_, ...), custom_call_target="tpu_custom_call" | custom-call | flops 2013265920 | bytes 5242880 | tf_op jit(solution)/shard_map/pallas_call | solution.py:66
  127.5 6.6 %shard_map.100 = (f32[512,256]{1,0:T(8,128)S(1)}, f32[512,256]{1,0:T(8,128)S(1)}) custom-call(s32[17]{0:T(128)S(1)} %stack.107.index.refs_0_, f32[2048,2048]{1,0:T(8,128)} %part.5, f32[512,768]{1,0:T(8,128)S(1)} %get-tuple-element.58.res_y.refs_17_, f32[512,1280]{1,0:T(8,128)S(1)} %get-tuple-element.60.res_z.refs_9_.refs_17_), custom_call_target="tpu_custom_call" | custom-call | flops 3221225472 | bytes 8388608 | tf_op jit(solution)/shard_map/pallas_call | solution.py:66
  140.4 3.3 %collective-permute-start.16 = (f32[64,768]{1,0:T(8,128)S(1)}, f32[64,768]{1,0:T(8,128)S(1)}, u32[]{:S(2)}, u32[]{:S(2)}) collective-permute-start(f32[64,768]{1,0:T(8,128)S(1)} %get-tuple-element.109), channel_id=1, source_target_pairs={{0,96},{32,0},{64,32},{96,64},{1,97},{33,1},{65,33},{97,65},{2,98}... | collective-permute-start | bytes 589832 | tf_op jit(solution)/shard_map/ppermute | solution.py:50
  143.7 2.9 %collective-permute-done.26 = f32[2,512,256]{2,1,0:T(8,128)S(1)} collective-permute-done((f32[2,512,256]{2,1,0:T(8,128)S(1)}, f32[2,512,256]{2,1,0:T(8,128)S(1)}, u32[]{:S(2)}, u32[]{:S(2)}) %collective-permute-start.26) | collective-permute-done | bytes 1048608 | tf_op jit(solution)/shard_map/ppermute | solution.py:50
  146.7 3.1 %collective-permute-done.24 = f32[2,512,256]{2,1,0:T(8,128)S(1)} collective-permute-done((f32[2,512,256]{2,1,0:T(8,128)S(1)}, f32[2,512,256]{2,1,0:T(8,128)S(1)}, u32[]{:S(2)}, u32[]{:S(2)}) %collective-permute-start.24) | collective-permute-done | bytes 1048608 | tf_op jit(solution)/shard_map/ppermute | solution.py:50
  153.7 13.5 %collective-permute-done.16 = f32[64,768]{1,0:T(8,128)S(1)} collective-permute-done((f32[64,768]{1,0:T(8,128)S(1)}, f32[64,768]{1,0:T(8,128)S(1)}, u32[]{:S(2)}, u32[]{:S(2)}) %collective-permute-start.16) | collective-permute-done | bytes 196640 | tf_op jit(solution)/shard_map/ppermute | solution.py:50
  167.2 4.2 %collective-permute-done.14 = f32[64,768]{1,0:T(8,128)S(1)} collective-permute-done((f32[64,768]{1,0:T(8,128)S(1)}, f32[64,768]{1,0:T(8,128)S(1)}, u32[]{:S(2)}, u32[]{:S(2)}) %collective-permute-start.14) | collective-permute-done | bytes 196640 | tf_op jit(solution)/shard_map/ppermute | solution.py:50
  183.4 3.0 %collective-permute-start.30 = (f32[1]{0:T(128)}, f32[1]{0:T(128)}, u32[]{:S(2)}, u32[]{:S(2)}) collective-permute-start(f32[1]{0:T(128)} %add.387), channel_id=1, source_target_pairs={{0,2},{1,3},{2,0},{3,1},{4,6},{5,7},{6,4},{7,5},{8,10},{9,11},{10,... | collective-permute-start | bytes 20 | tf_op jit(solution)/shard_map/ppermute | solution.py:56
  196.0 3.0 %collective-permute-start.32 = (f32[1]{0:T(128)}, f32[1]{0:T(128)}, u32[]{:S(2)}, u32[]{:S(2)}) collective-permute-start(f32[1]{0:T(128)} %add.389), channel_id=1, source_target_pairs={{0,64},{32,96},{64,0},{96,32},{1,65},{33,97},{65,1},{97,33},{2,66}... | collective-permute-start | bytes 20 | tf_op jit(solution)/shard_map/ppermute | solution.py:56
  (118 shorter events, 76.0 us)
Async XLA Ops:
  9.5 16.7 %collective-permute-start.3 = (f32[2,264,256]{2,1,0:T(8,128)S(1)}, f32[2,264,256]{2,1,0:T(8,128)S(1)}, u32[]{:S(2)}, u32[]{:S(2)}) collective-permute-start(f32[2,264,256]{2,1,0:T(8,128)S(1)} %shard_map.84.refs_1_.refs_5_.refs_8_), channel_id=1, source_target_pairs={{0,2},{1,3},{2,0},{3,1},{4,6},{5,7},{6,4},{7,5},{8,10},{9,11},{10,... | collective-permute-start | bytes 1622024 | tf_op jit(solution)/shard_map/ppermute | solution.py:50
  12.5 25.3 %collective-permute-start.2 = (f32[2,264,256]{2,1,0:T(8,128)S(1)}, f32[2,264,256]{2,1,0:T(8,128)S(1)}, u32[]{:S(2)}, u32[]{:S(2)}) collective-permute-start(f32[2,264,256]{2,1,0:T(8,128)S(1)} %shard_map.84.refs_1_.refs_5_.refs_8_), channel_id=1, source_target_pairs={{0,3},{1,0},{2,1},{3,2},{4,7},{5,4},{6,5},{7,6},{8,11},{9,8},{10,9... | collective-permute-start | bytes 1622024 | tf_op jit(solution)/shard_map/ppermute | solution.py:50
  13.6 24.2 %collective-permute-start.1 = (f32[2,264,256]{2,1,0:T(8,128)S(1)}, f32[2,264,256]{2,1,0:T(8,128)S(1)}, u32[]{:S(2)}, u32[]{:S(2)}) collective-permute-start(f32[2,264,256]{2,1,0:T(8,128)S(1)} %shard_map.84.refs_1_.refs_5_.refs_8_), channel_id=1, source_target_pairs={{0,1},{1,2},{2,3},{3,0},{4,5},{5,6},{6,7},{7,4},{8,9},{9,10},{10,1... | collective-permute-start | bytes 1622024 | tf_op jit(solution)/shard_map/ppermute | solution.py:50
  21.7 26.3 %collective-permute-start.5 = (f32[2,264,256]{2,1,0:T(8,128)S(1)}, f32[2,264,256]{2,1,0:T(8,128)S(1)}, u32[]{:S(2)}, u32[]{:S(2)}) collective-permute-start(f32[2,264,256]{2,1,0:T(8,128)S(1)} %collective-permute-done.refs_1_.refs_12_.refs_5_), channel_id=1, source_target_pairs={{0,3},{1,0},{2,1},{3,2},{4,7},{5,4},{6,5},{7,6},{8,11},{9,8},{10,9... | collective-permute-start | bytes 1622024 | tf_op jit(solution)/shard_map/ppermute | solution.py:50
  24.6 23.5 %collective-permute-start.4 = (f32[2,264,256]{2,1,0:T(8,128)S(1)}, f32[2,264,256]{2,1,0:T(8,128)S(1)}, u32[]{:S(2)}, u32[]{:S(2)}) collective-permute-start(f32[2,264,256]{2,1,0:T(8,128)S(1)} %collective-permute-done.refs_1_.refs_12_.refs_5_), channel_id=1, source_target_pairs={{0,1},{1,2},{2,3},{3,0},{4,5},{5,6},{6,7},{7,4},{8,9},{9,10},{10,1... | collective-permute-start | bytes 1622024 | tf_op jit(solution)/shard_map/ppermute | solution.py:50
  26.2 21.7 %collective-permute-start.6 = (f32[2,264,256]{2,1,0:T(8,128)S(1)}, f32[2,264,256]{2,1,0:T(8,128)S(1)}, u32[]{:S(2)}, u32[]{:S(2)}) collective-permute-start(f32[2,264,256]{2,1,0:T(8,128)S(1)} %collective-permute-done.3.refs_3_.refs_7_.refs_9_), channel_id=1, source_target_pairs={{0,4},{4,0},{1,5},{5,1},{2,6},{6,2},{3,7},{7,3},{8,12},{12,8},{9,1... | collective-permute-start | bytes 1622024 | tf_op jit(solution)/shard_map/ppermute | solution.py:50
  63.9 20.0 %collective-permute-start.9 = (f32[512,1280]{1,0:T(8,128)S(1)}, f32[512,1280]{1,0:T(8,128)S(1)}, u32[]{:S(2)}, u32[]{:S(2)}) collective-permute-start(f32[512,1280]{1,0:T(8,128)S(1)} %get-tuple-element.60.res_z.refs_9_.refs_17_), channel_id=1, source_target_pairs={{0,8},{8,0},{1,9},{9,1},{2,10},{10,2},{3,11},{11,3},{4,12},{12,4},... | collective-permute-start | bytes 7864328 | tf_op jit(solution)/shard_map/ppermute | solution.py:50
  64.0 26.1 %collective-permute-start.12 = (f32[512,768]{1,0:T(8,128)S(1)}, f32[512,768]{1,0:T(8,128)S(1)}, u32[]{:S(2)}, u32[]{:S(2)}) collective-permute-start(f32[512,768]{1,0:T(8,128)S(1)} %get-tuple-element.58.res_y.refs_17_), channel_id=1, source_target_pairs={{0,8},{8,0},{1,9},{9,1},{2,10},{10,2},{3,11},{11,3},{4,12},{12,4},... | collective-permute-start | bytes 4718600 | tf_op jit(solution)/shard_map/ppermute | solution.py:50
  65.5 17.2 %collective-permute-start.8 = (f32[4,512,128]{2,1,0:T(8,128)S(1)}, f32[4,512,128]{2,1,0:T(8,128)S(1)}, u32[]{:S(2)}, u32[]{:S(2)}) collective-permute-start(f32[4,512,128]{2,1,0:T(8,128)S(1)} %get-tuple-element.66), channel_id=1, source_target_pairs={{0,8},{8,0},{1,9},{9,1},{2,10},{10,2},{3,11},{11,3},{4,12},{12,4},... | collective-permute-start | bytes 3145736 | tf_op jit(solution)/shard_map/ppermute | solution.py:50
  78.7 46.4 %collective-permute-start.23 = (f32[512,256]{1,0:T(8,128)S(1)}, f32[512,256]{1,0:T(8,128)}, u32[]{:S(2)}, u32[]{:S(2)}) collective-permute-start(f32[512,256]{1,0:T(8,128)S(1)} %get-tuple-element.68), channel_id=1, source_target_pairs={{0,1},{1,2},{2,3},{3,0},{4,5},{5,6},{6,7},{7,4},{8,9},{9,10},{10,1... | collective-permute-start | bytes 1572872 | tf_op jit(solution)/shard_map/ppermute | solution.py:50
  80.8 42.1 %collective-permute-start.25 = (f32[512,256]{1,0:T(8,128)S(1)}, f32[512,256]{1,0:T(8,128)}, u32[]{:S(2)}, u32[]{:S(2)}) collective-permute-start(f32[512,256]{1,0:T(8,128)S(1)} %get-tuple-element.98), channel_id=1, source_target_pairs={{0,3},{1,0},{2,1},{3,2},{4,7},{5,4},{6,5},{7,6},{8,11},{9,8},{10,9... | collective-permute-start | bytes 1572872 | tf_op jit(solution)/shard_map/ppermute | solution.py:50
  88.1 49.4 %collective-permute-start.18 = (f32[128,1280]{1,0:T(8,128)S(1)}, f32[128,1280]{1,0:T(8,128)}, u32[]{:S(2)}, u32[]{:S(2)}) collective-permute-start(f32[128,1280]{1,0:T(8,128)S(1)} %get-tuple-element.72), channel_id=1, source_target_pairs={{0,32},{32,64},{64,96},{96,0},{1,33},{33,65},{65,97},{97,1},{2,34}... | collective-permute-start | bytes 1966088 | tf_op jit(solution)/shard_map/ppermute | solution.py:50
  94.1 45.0 %collective-permute-start.13 = (f32[4,128,768]{2,1,0:T(8,128)S(1)}, f32[4,128,768]{2,1,0:T(8,128)}, u32[]{:S(2)}, u32[]{:S(2)}) collective-permute-start(f32[4,128,768]{2,1,0:T(8,128)S(1)} %shard_map.95), channel_id=1, source_target_pairs={{0,16},{16,0},{1,17},{17,1},{2,18},{18,2},{3,19},{19,3},{4,20},{20... | collective-permute-start | bytes 4718600 | tf_op jit(solution)/shard_map/ppermute | solution.py:50
  95.7 38.4 %collective-permute-start.20 = (f32[128,1280]{1,0:T(8,128)S(1)}, f32[128,1280]{1,0:T(8,128)}, u32[]{:S(2)}, u32[]{:S(2)}) collective-permute-start(f32[128,1280]{1,0:T(8,128)S(1)} %get-tuple-element.93), channel_id=1, source_target_pairs={{0,96},{32,0},{64,32},{96,64},{1,97},{33,1},{65,33},{97,65},{2,98}... | collective-permute-start | bytes 1966088 | tf_op jit(solution)/shard_map/ppermute | solution.py:50
  124.1 22.5 %collective-permute-start.26 = (f32[2,512,256]{2,1,0:T(8,128)S(1)}, f32[2,512,256]{2,1,0:T(8,128)S(1)}, u32[]{:S(2)}, u32[]{:S(2)}) collective-permute-start(f32[2,512,256]{2,1,0:T(8,128)S(1)} %pad_maximum_fusion.3), channel_id=1, source_target_pairs={{0,3},{1,0},{2,1},{3,2},{4,7},{5,4},{6,5},{7,6},{8,11},{9,8},{10,9... | collective-permute-start | bytes 3145736 | tf_op jit(solution)/shard_map/ppermute | solution.py:50
  126.3 23.4 %collective-permute-start.24 = (f32[2,512,256]{2,1,0:T(8,128)S(1)}, f32[2,512,256]{2,1,0:T(8,128)S(1)}, u32[]{:S(2)}, u32[]{:S(2)}) collective-permute-start(f32[2,512,256]{2,1,0:T(8,128)S(1)} %pad_maximum_fusion.2), channel_id=1, source_target_pairs={{0,1},{1,2},{2,3},{3,0},{4,5},{5,6},{6,7},{7,4},{8,9},{9,10},{10,1... | collective-permute-start | bytes 3145736 | tf_op jit(solution)/shard_map/ppermute | solution.py:50
  135.3 39.7 %collective-permute-start.21 = (f32[2,128,1280]{2,1,0:T(8,128)S(1)}, f32[2,128,1280]{2,1,0:T(8,128)S(1)}, u32[]{:S(2)}, u32[]{:S(2)}) collective-permute-start(f32[2,128,1280]{2,1,0:T(8,128)S(1)} %pad_maximum_fusion.1), channel_id=1, source_target_pairs={{0,96},{32,0},{64,32},{96,64},{1,97},{33,1},{65,33},{97,65},{2,98}... | collective-permute-start | bytes 3932168 | tf_op jit(solution)/shard_map/ppermute | solution.py:50
  138.7 36.4 %collective-permute-start.19 = (f32[2,128,1280]{2,1,0:T(8,128)S(1)}, f32[2,128,1280]{2,1,0:T(8,128)S(1)}, u32[]{:S(2)}, u32[]{:S(2)}) collective-permute-start(f32[2,128,1280]{2,1,0:T(8,128)S(1)} %pad_maximum_fusion), channel_id=1, source_target_pairs={{0,32},{32,64},{64,96},{96,0},{1,33},{33,65},{65,97},{97,1},{2,34}... | collective-permute-start | bytes 3932168 | tf_op jit(solution)/shard_map/ppermute | solution.py:50
  140.4 26.7 %collective-permute-start.16 = (f32[64,768]{1,0:T(8,128)S(1)}, f32[64,768]{1,0:T(8,128)S(1)}, u32[]{:S(2)}, u32[]{:S(2)}) collective-permute-start(f32[64,768]{1,0:T(8,128)S(1)} %get-tuple-element.109), channel_id=1, source_target_pairs={{0,96},{32,0},{64,32},{96,64},{1,97},{33,1},{65,33},{97,65},{2,98}... | collective-permute-start | bytes 589832 | tf_op jit(solution)/shard_map/ppermute | solution.py:50
  146.7 24.7 %collective-permute-start.14 = (f32[64,768]{1,0:T(8,128)S(1)}, f32[64,768]{1,0:T(8,128)S(1)}, u32[]{:S(2)}, u32[]{:S(2)}) collective-permute-start(f32[64,768]{1,0:T(8,128)S(1)} %get-tuple-element.110), channel_id=1, source_target_pairs={{0,32},{32,64},{64,96},{96,0},{1,33},{33,65},{65,97},{97,1},{2,34}... | collective-permute-start | bytes 589832 | tf_op jit(solution)/shard_map/ppermute | solution.py:50
  150.8 38.5 %collective-permute-start.27 = (f32[512,256]{1,0:T(8,128)}, f32[512,256]{1,0:T(8,128)}, u32[]{:S(2)}, u32[]{:S(2)}) collective-permute-start(f32[512,256]{1,0:T(8,128)} %fusion.7), channel_id=1, source_target_pairs={{0,4},{4,0},{1,5},{5,1},{2,6},{6,2},{3,7},{7,3},{8,12},{12,8},{9,1... | collective-permute-start | bytes 1572872 | tf_op jit(solution)/shard_map/ppermute | solution.py:50
  172.3 19.4 %collective-permute-start.17 = (f32[128,768]{1,0:T(8,128)}, f32[128,768]{1,0:T(8,128)}, u32[]{:S(2)}, u32[]{:S(2)}) collective-permute-start(f32[128,768]{1,0:T(8,128)} %pad_maximum_fusion.5), channel_id=1, source_target_pairs={{0,96},{32,0},{64,32},{96,64},{1,97},{33,1},{65,33},{97,65},{2,98}... | collective-permute-start | bytes 1179656 | tf_op jit(solution)/shard_map/ppermute | solution.py:50
  173.1 18.6 %collective-permute-start.15 = (f32[128,768]{1,0:T(8,128)}, f32[128,768]{1,0:T(8,128)}, u32[]{:S(2)}, u32[]{:S(2)}) collective-permute-start(f32[128,768]{1,0:T(8,128)} %pad_maximum_fusion.4), channel_id=1, source_target_pairs={{0,32},{32,64},{64,96},{96,0},{1,33},{33,65},{65,97},{97,1},{2,34}... | collective-permute-start | bytes 1179656 | tf_op jit(solution)/shard_map/ppermute | solution.py:50
  176.9 25.0 %collective-permute-start.22 = (f32[128,1280]{1,0:T(8,128)}, f32[128,1280]{1,0:T(8,128)}, u32[]{:S(2)}, u32[]{:S(2)}) collective-permute-start(f32[128,1280]{1,0:T(8,128)} %fusion.2), channel_id=1, source_target_pairs={{0,16},{16,0},{1,17},{17,1},{2,18},{18,2},{3,19},{19,3},{4,20},{20... | collective-permute-start | bytes 1966088 | tf_op jit(solution)/shard_map/ppermute | solution.py:50
  (28 other events, 219.5 us)

commit v2 on v0

v2 whole, which is shorter than its diff:
```python
import functools

import jax
import jax.numpy as jnp
from jax import lax
from jax.experimental import pallas as pl
from jax.experimental.pallas import tpu as pltpu
from jax.sharding import Mesh
from jax.sharding import PartitionSpec as P

DT = 16384
TOKENS = 8192
TOK = ("tok_0", "tok_1", "tok_2")
FEAT = ("feat_0", "feat_1")
Z, YLO, CORE, YHI, X = "tok_0", "tok_1", "tok_2", "feat_0", "feat_1"

norm_eps = 1e-05
momentum_rate = 0.9
step_rate = 0.5


F32, BF16 = jnp.float32, jnp.bfloat16
CY = 768
TN = 256
MIB = 1 << 20


def halves(value):
    hi = value.astype(BF16)
    return hi, (value - hi.astype(F32)).astype(BF16)


def dot(a, b, dims):
    return lax.dot_general(a, b, (dims, ((), ())), preferred_element_type=F32)


def shift(value, axis, by, size):
    return lax.ppermute(value, axis, [(i, (i + by) % size) for i in range(size)])


def sum_pair(value, axis, far=False):
    size = lax.axis_size(axis)
    step = 2 if far else 1
    return value + lax.ppermute(value, axis, [(i, i ^ step) for i in range(size)])


def after(index, *earlier):
    return lax.optimization_barrier((index, *earlier))[0]


def kernel(body, index, args, out_shape, flops, scratch=(), vmem=8):
    specs = [pl.BlockSpec(memory_space=pltpu.SMEM)]
    specs += [pl.BlockSpec(memory_space=pltpu.VMEM)] * len(args)
    return pl.pallas_call(
        body,
        in_specs=specs,
        out_specs=[pl.BlockSpec(memory_space=pltpu.VMEM)] * len(out_shape),
        out_shape=out_shape,
        scratch_shapes=scratch,
        cost_estimate=pl.CostEstimate(flops=flops, bytes_accessed=MIB, transcendentals=0),
        compiler_params=pltpu.CompilerParams(vmem_limit_bytes=vmem * MIB),
    )(index, *args)


def of(shape, kind=F32):
    return jax.ShapeDtypeStruct(shape, kind)


FEATURE = {(dy, dx): dy * 4 + dx for dy in (0, 1) for dx in range(4)}
SLOT = {(dz, dy): 8 + dz * 2 + dy for dz in range(4) for dy in (0, 1)}
CORE_AT = 16


def table():
    z, ylo, core = lax.axis_index(Z), lax.axis_index(YLO), lax.axis_index(CORE)
    yhi, x = lax.axis_index(YHI), lax.axis_index(X)
    entries = [(yhi ^ dy) * 4 + (x + dx) % 4 for dy, dx in FEATURE]
    for dz, dy in SLOT:
        index = ((z + dz) % 4) * 2 + (ylo ^ dy)
        entries.append(((index // 4) ^ yhi) * 4 + (index % 4 - x) % 4)
    entries.append(core)
    return jnp.stack(entries).astype(jnp.int32)


EXTRA = 8


def packed(teacher, student):
    rows, width = student.shape
    sums = jnp.sum(teacher * teacher, axis=1).reshape(2, 1, rows // 2)
    sums = jnp.broadcast_to(sums, (2, EXTRA, rows // 2))
    return jnp.concatenate([student.reshape(2, rows // 2, width), sums], 1)


def forward_body(at, first, tiles, per, with_acc, final, index, *refs):
    refs = list(refs)
    count = len(at)
    blocks = [refs.pop(0) for _ in range(count)]
    projector = refs.pop(0)
    acc = refs.pop(0) if with_acc else None
    left = refs.pop()
    half = blocks[0].shape[1] - EXTRA
    width = blocks[0].shape[2]
    for k in range(count):
        for h in (0, 1):
            rows = pl.ds(h * half, half)
            for part, value in enumerate(halves(blocks[k][h, :half, :])):
                left[rows, pl.ds((2 * k + part) * width, width)] = value
    if final:
        sums = [refs.pop(0) for _ in range(8)]
        partial = [s[:, half:, :] for s in sums]
        while len(partial) > 1:
            partial = [p + q for p, q in zip(partial[::2], partial[1::2])]
        scale = lax.rsqrt(partial[0] / DT + norm_eps)
        scale = jnp.concatenate([scale[0].T, scale[1].T], 0)[:, :1]
        teacher, gain, out, out_hi, out_lo, error, column = refs
        column[...] = jnp.broadcast_to(scale, column.shape)
        error[...] = jnp.zeros_like(error)

    def product(cols):
        total = None
        for k in range(count):
            start = pl.multiple_of(index[at[k]] * width, width)
            b_hi, b_lo = halves(projector[pl.ds(start, width), cols])
            a_hi = left[:, pl.ds(2 * k * width, width)]
            a_lo = left[:, pl.ds((2 * k + 1) * width, width)]
            for a, b in ((a_hi, b_hi), (a_lo, b_hi), (a_hi, b_lo)):
                term = dot(a, b, ((1,), (0,)))
                total = term if total is None else total + term
        return total

    def step(j, carry):
        for p in range(per):
            here = pl.multiple_of((j * per + p) * TN, TN)
            there = pl.ds(here + first * TN, TN)
            here = pl.ds(here, TN)
            total = product(there)
            if with_acc:
                total = total + acc[:, there]
            if final:
                wide = jnp.concatenate([column[...]] * (TN // 128), 1)
                total = total - (teacher[:, there] * wide) * gain[:, there]
                out_hi[:, here], out_lo[:, here] = halves(total)
                out[:, here] = total
                error[...] += jnp.sum((total * total).reshape(-1, 8, TN), axis=0)
            else:
                refs[0][:, here] = total
        return carry

    lax.fori_loop(0, tiles // per, step, 0)


def forward(index, pieces, at, projector, acc=None, final=None, first=0, tiles=8, per=2):
    count = len(pieces)
    width = pieces[0].shape[2]
    rows = 2 * (pieces[0].shape[1] - EXTRA)
    args = [*pieces, projector]
    if acc is not None:
        args.append(acc)
    out = [of((rows, TN * tiles))]
    scratch = [pltpu.VMEM((rows, 2 * count * width), BF16)]
    if final is not None:
        every, teacher, gain = final
        args += [*every, teacher, gain]
        out += [of((rows, TN * tiles), BF16)] * 2 + [of((8, TN))]
        scratch.insert(0, pltpu.VMEM((rows, 128), F32))
    result = kernel(
        functools.partial(forward_body, at, first, tiles, per, acc is not None, final is not None),
        index,
        args,
        out,
        6 * rows * width * count * TN * tiles,
        scratch,
    )
    return result if final is not None else result[0]


def prepare_body(slots, kept, index, *refs):
    refs = list(refs)
    blocks = [refs.pop(0) for _ in slots]
    if kept:
        old_hi, old_lo = refs.pop(0), refs.pop(0)
    hi, lo, sent = refs
    half, width = blocks[0].shape[1] - EXTRA, blocks[0].shape[2] // 2
    for k in kept:
        hi[k] = old_hi[k]
        lo[k] = old_lo[k]
    mine = pl.ds(pl.multiple_of(index[CORE_AT] * width, width), width)
    theirs = pl.ds(pl.multiple_of((1 - index[CORE_AT]) * width, width), width)
    for k, slot in enumerate(slots):
        for h in (0, 1):
            rows = pl.ds(h * half, half)
            a, b = halves(blocks[k][h, :half, mine].T)
            hi[slot, :, rows] = a
            lo[slot, :, rows] = b
            sent[k, rows, :] = blocks[k][h, :half, theirs]


def prepare(index, pieces, slots, old=None):
    _, long, width = pieces[0].shape
    rows = 2 * (long - EXTRA)
    kept = () if old is None else tuple(k for k in range(8) if k not in slots)
    split = of((8, width // 2, rows), BF16)
    return kernel(
        functools.partial(prepare_body, slots, kept),
        index,
        [*pieces, *(old or ())],
        [split, split, of((len(pieces), rows, width // 2))],
        MIB,
    )


def turn_body(slots, index, first, second, hi, lo):
    for part, where in zip((first, second), slots):
        for k, slot in enumerate(where):
            a, b = halves(part[k].T)
            hi[slot], lo[slot] = a, b


def turned(index, came, slots):
    _, rows, width = came[0].shape
    split = of((8, width, rows), BF16)
    return kernel(functools.partial(turn_body, slots), index, came, [split, split], MIB)


def grad_body(at, places, adds, index, *refs):
    refs = list(refs)
    splits = [refs.pop(0) for _ in range(4)]
    mine_hi, mine_lo, other = (refs.pop(0) for _ in range(3))
    added = [refs.pop(0) for _ in adds]
    left, outs = refs.pop(), refs
    _, rows, tokens = splits[0].shape
    for k in range(len(at)):
        for part in range(4):
            where = pl.ds(k * rows, rows), pl.ds(part * tokens, tokens)
            left[where] = splits[part][index[at[k]]]

    def step(j, carry):
        cols = pl.ds(pl.multiple_of(j * TN, TN), TN)
        a_hi, a_lo, b_hi, b_lo = (left[:, pl.ds(p * tokens, tokens)] for p in range(4))
        own_hi, own_lo = mine_hi[:, cols], mine_lo[:, cols]
        oth_hi, oth_lo = halves(other[:, cols])
        total = None
        for a, b in (
            (a_hi, own_hi),
            (a_lo, own_hi),
            (a_hi, own_lo),
            (b_hi, oth_hi),
            (b_lo, oth_hi),
            (b_hi, oth_lo),
        ):
            term = dot(a, b, ((1,), (0,)))
            total = term if total is None else total + term
        for k, (out, row) in enumerate(places):
            value = total[k * rows : (k + 1) * rows]
            for (which, source), ref in zip(adds, added):
                if which == k:
                    value = value + (ref[:, cols] if source is None else ref[source, :, cols])
            if row is None:
                outs[out][:, cols] = value
            else:
                outs[out][row, :, cols] = value
        return carry

    lax.fori_loop(0, other.shape[1] // TN, step, 0)


def outputs_of(places, shape):
    out = []
    for k in range(1 + max(o for o, _ in places)):
        depth = sum(o == k for o, _ in places)
        single = any(o == k and r is None for o, r in places)
        out.append(of(shape if single else (depth, *shape)))
    return out


def grad_blocks(index, at, places, splits, mine, other, adds=()):
    _, rows, tokens = splits[0].shape
    cols = other.shape[1]
    which = tuple((k, row) for k, row, _ in adds)
    return kernel(
        functools.partial(grad_body, at, places, which),
        index,
        [*splits, *mine, other, *[array for _, _, array in adds]],
        outputs_of(places, (rows, cols)),
        12 * rows * len(at) * tokens * cols,
        [pltpu.VMEM((len(at) * rows, 4 * tokens), BF16)],
    )


def state_body(at, places, adds, split_at, width, index, projector, *refs):
    refs = list(refs)
    his = [refs.pop(0) for _ in range(2)]
    los = [refs.pop(0) for _ in range(2)]
    added = [refs.pop(0) for _ in adds]
    outs = refs
    cuts = (slice(0, split_at), slice(split_at, projector.shape[1]))
    for k, (out, row) in enumerate(places):
        rows = pl.ds(pl.multiple_of(index[at[k]] * width, width), width)
        total = None
        for cut, hi, lo in zip(cuts, his, los):
            w_hi, w_lo = halves(projector[rows, cut])
            for a, b in ((hi, w_hi), (lo, w_hi), (hi, w_lo)):
                term = dot(a[...], b, ((1,), (1,)))
                total = term if total is None else total + term
        for which, ref in zip(adds, added):
            if which == k:
                total = total + ref[...]
        if row is None:
            outs[out][...] = total
        else:
            outs[out][row] = total


def state_blocks(index, at, places, projector, his, los, adds=()):
    rows, split_at = his[0].shape
    width = 256
    which = tuple(k for k, _ in adds)
    return kernel(
        functools.partial(state_body, at, places, which, split_at, width),
        index,
        [projector, *his, *los, *[array for _, array in adds]],
        outputs_of(places, (rows, width)),
        6 * rows * len(at) * width * projector.shape[1],
    )


def in_layer(teacher, student, gain, projector, momentum):
    _, cols = teacher.shape
    width = student.shape[1]
    half = width // 2
    index = table()

    def at(*pairs):
        return [FEATURE[p] for p in pairs]

    own = packed(teacher, student)
    upper = shift(own, YHI, 1, 2)
    left, right = shift(own, X, 1, 4), shift(own, X, -1, 4)
    far = shift(own, X, 2, 4)
    acc = forward(index, [own], at((0, 0)), projector)
    acc = forward(after(index, acc), [upper], at((1, 0)), projector, acc)
    ul, ur = shift(upper, X, 1, 4), shift(upper, X, -1, 4)
    ufar = shift(far, YHI, 1, 2)
    acc = forward(after(index, acc), [left, right, far], at((0, 3), (0, 1), (0, 2)), projector, acc)
    hi, lo, sent_a = prepare(after(index, acc), [own, right, far, left], (0, 1, 2, 3))
    came_a = shift(sent_a, CORE, 1, 2)
    hi, lo, sent_b = prepare(after(index, sent_a), [upper, ur, ufar, ul], (4, 5, 6, 7), (hi, lo))
    came_b = shift(sent_b, CORE, 1, 2)
    every = [own, far, left, right, upper, ufar, ul, ur]
    args = ([ul, ur, ufar], at((1, 3), (1, 1), (1, 2)), projector, acc)
    args += ((every, teacher, gain.reshape(1, cols)),)
    res_z, *res_z_split, err_z = forward(
        after(index, sent_b), *args, CY // TN, (cols - CY) // TN, 1
    )
    other_z = shift(res_z, CORE, 1, 2)
    res_y, *res_y_split, err_y = forward(after(index, res_z), *args, 0, CY // TN, 1)
    other_y = shift(res_y, CORE, 1, 2)
    error = jnp.sum(err_y + err_z).reshape(1)
    error = sum_pair(error, Z)
    splits = (
        hi,
        lo,
        *turned(after(index, res_y), (came_a, came_b), ((0, 1, 2, 3), (4, 5, 6, 7))),
    )

    def state(index, pairs, places, adds=()):
        his, los = zip(res_y_split, res_z_split)
        return state_blocks(index, at(*pairs), places, projector, his, los, adds)

    def grad_y(index, pairs, places, adds=()):
        slots = [SLOT[p] for p in pairs]
        return grad_blocks(index, slots, places, splits, res_y_split, other_y, adds)

    def grad_z(index, pairs, places, adds=()):
        slots = [SLOT[p] for p in pairs]
        return grad_blocks(index, slots, places, splits, res_z_split, other_z, adds)

    apart = ((0, None), (1, None))
    paired = ((0, 0), (0, 1), (1, 0), (1, 1))
    sfar = state(after(index, splits[2]), ((0, 2), (1, 2)), apart)
    sfo, sft = shift(sfar[0], X, 1, 4), shift(sfar[1], X, -1, 4)
    error = sum_pair(after(error, sfar[0]), Z, far=True)
    zfar = grad_z(after(index, sfar[0]), ((2, 0), (2, 1)), apart)
    zfo, zft = shift(zfar[0], Z, 1, 4), shift(zfar[1], Z, -1, 4)
    error = sum_pair(after(error, zfar[0]), YLO)
    (ys,) = grad_y(
        after(index, zfar[0]), ((2, 1), (1, 1), (3, 1), (0, 1)), ((0, 0), (0, 1), (0, 2), (0, 3))
    )
    error = sum_pair(after(error, ys), YHI)
    zero = grad_z(after(index, ys), ((0, 0), (0, 1)), apart)
    ys, error, _ = lax.optimization_barrier((ys, error, zero[0]))
    ys = shift(ys, YLO, 1, 2)
    sup, sdown = state(
        after(index, zero[0]), ((0, 1), (1, 1), (0, 3), (1, 3)), paired, ((0, sfo), (3, sft))
    )
    sup_came, sdown_came = shift(sup, X, 1, 4), shift(sdown, X, -1, 4)
    up, down = grad_z(
        after(index, sup),
        ((1, 0), (1, 1), (3, 0), (3, 1)),
        paired,
        ((0, None, zfo), (3, None, zft)),
    )
    up_came, down_came = shift(up, Z, 1, 4), shift(down, Z, -1, 4)
    error = sum_pair(after(error, up), CORE)
    s0 = state(after(index, up), ((0, 0), (1, 0)), apart)
    two, one, three, rest = grad_y(
        after(index, s0[0]),
        ((2, 0), (1, 0), (3, 0), (0, 0)),
        ((0, None), (1, None), (2, None), (3, None)),
        tuple((k, k, ys) for k in range(4)),
    )
    s_part = s0[1] + (sup_came[1] + sdown_came[1])
    s_part, _ = lax.optimization_barrier((s_part, rest))
    s_came = shift(s_part, YHI, 1, 2)
    error = sum_pair(after(error, s_part), X)
    error = sum_pair(error, X, far=True)
    z_part = zero[1] + (up_came[1] + down_came[1])
    z_part, error, _ = lax.optimization_barrier((z_part, error, s_part))
    two, one, three, _ = lax.optimization_barrier((two, one, three, z_part))
    y2 = shift(two, Z, 2, 4)
    y1, y3 = shift(one, Z, 1, 4), shift(three, Z, -1, 4)
    z_came = shift(z_part, YLO, 1, 2)
    grad_hi = (zero[0] + (up_came[0] + down_came[0])) + z_came
    grad_lo = (rest + y2) + (y1 + y3)
    proj_grad = jnp.concatenate([grad_lo, grad_hi], 1) / TOKENS
    student_grad = (s0[0] + (sup_came[0] + sdown_came[0])) + s_came
    loss_value = error[0] / (TOKENS * DT)

    new_momentum = momentum_rate * momentum + proj_grad
    own_block = lax.axis_index(Z) * 4 + lax.axis_index(YLO) * 2 + lax.axis_index(CORE)
    own_rows = lax.dynamic_slice_in_dim(projector, own_block * half, half, 0)
    new_projector = own_rows - step_rate * new_momentum
    return (new_projector, new_momentum, student_grad, loss_value)


def solution(mesh):
    split = Mesh(
        mesh.devices.reshape(4, 2, 2, 2, 4), ("tok_0", "tok_1", "tok_2", "feat_0", "feat_1")
    )
    in_specs = (P(TOK, FEAT), P(TOK, FEAT), P(FEAT), P(None, FEAT), P(TOK, FEAT))
    out_specs = (P(TOK, FEAT), P(TOK, FEAT), P(TOK, FEAT), P())
    return jax.shard_map(
        in_layer, mesh=split, in_specs=in_specs, out_specs=out_specs, check_vma=False
    )
```

time: 396 us -> 185 us (0.47)
  waiting for transfers between devices: 158 us -> 36.7 us
  blocking collectives: 104 us -> 0 us
  matrix products: 94.6 us -> 0 us
  Pallas kernels: 0 us -> 64.1 us
  starting transfers between devices: 4.62 us -> 52.1 us
  between operations: 15.9 us -> 7.27 us
  other arithmetic: 8.28 us -> 13 us
    psum x6 -> x0, blocking collectives: 104 us -> none  [the longest x5 79.2 us: over_axes(): value = lax.psum(value, axis)]
    reduce_scatter x1 -> x0, waiting for transfers between devices: 102 us -> none  [on_device(): lax.psum_scatter(lax.dot_general(full_student, residual, (((0,), (0,)), (...]
    dot_general x3 -> x0, matrix products: 94.6 us -> none  [the longest x1 32.5 us: on_device(): jnp.dot(full_student, projector, precision=highest, preferred_element_typ...]
    pallas_call x0 -> x16, Pallas kernels: none -> 64.1 us  [kernel(): pl.pallas_call(body, in_specs=specs, out_specs=[pl.BlockSpec(memory_space...]
    all_gather x1 -> x0, waiting for transfers between devices: 54.8 us -> none  [on_device(): full_student = lax.all_gather(student, FEAT, axis=1, tiled=True)]
    ppermute x0 -> x32, starting transfers between devices: none -> 52.1 us  [the longest x25 34.4 us: shift(): lax.ppermute(value, axis, [(i, (i + by) % size) for i in range(size)])]
    ppermute x0 -> x32, waiting for transfers between devices: none -> 36.7 us  [the longest x25 28.7 us: shift(): lax.ppermute(value, axis, [(i, (i + by) % size) for i in range(size)])]
    add x0 -> x5, other arithmetic: none -> 6.89 us  [the longest x1 2.23 us: in_layer(): student_grad = s0[0] + (sup_came[0] + sdown_came[0]) + s_came]
  transfers between devices with their start and end apart: 3 -> 32, of which waited for: 2 -> 12; matrix products, arithmetic and copies ran while one was open for 11% -> 3% of each run, Pallas kernels for 0% -> 31%
where the time goes in v2:
time: 185 us; the launch traced here: 183 us
  Pallas kernels  64.1 us (35%)
  starting transfers between devices  52.1 us (28%)
  waiting for transfers between devices  36.7 us (20%)
  other arithmetic  13 us (7%)
  local copies, waits for them, and re-layouts  10 us (5%)
  between operations  7.27 us (4%)
    pallas_call x16, Pallas kernels, kernel(): pl.pallas_call(body, in_specs=specs, out_specs=[pl.BlockSpec(memory_space...  64.1 us
    ppermute x25, starting transfers between devices, shift(): lax.ppermute(value, axis, [(i, (i + by) % size) for i in range(size)])  34.4 us
    ppermute x25, waiting for transfers between devices, shift(): lax.ppermute(value, axis, [(i, (i + by) % size) for i in range(size)])  28.7 us
    ppermute x7, starting transfers between devices, sum_pair(): lax.ppermute(value, axis, [(i, i ^ step) for i in range(size)])  17.7 us
    unnamed x44, local copies, waits for them, and re-layouts  9.93 us
    ppermute x7, waiting for transfers between devices, sum_pair(): lax.ppermute(value, axis, [(i, i ^ step) for i in range(size)])  7.95 us
  transfers between devices with their start and end apart: 32, of which 12 were waited for; matrix products, arithmetic and copies ran while one was open for 3% of the time, Pallas kernels for 31%

profile of v2, /device:TPU:0, one launch (start us, length us, event | category | flops | bytes accessed | tf_op | source)
XLA Modules:
  0.0 183.2 jit_solution(7141766937090829609)
XLA Ops:
  3.3 3.4 %collective-permute-start = (f32[2,264,256]{2,1,0:T(8,128)S(1)}, f32[2,264,256]{2,1,0:T(8,128)S(1)}, u32[]{:S(2)}, u32[]{:S(2)}) collective-permute-start(f32[2,264,256]{2,1,0:T(8,128)S(1)} %pad_maximum_fusion.refs_0_.refs_5_), channel_id=1, source_target_pairs={{0,4},{4,0},{1,5},{5,1},{2,6},{6,2},{3,7},{7,3},{8,12},{12,8},{9,1... | collective-permute-start | bytes 1622024 | tf_op jit(solution)/shard_map/ppermute | solution.py:38
  6.7 3.0 %collective-permute-start.3 = (f32[2,264,256]{2,1,0:T(8,128)S(1)}, f32[2,264,256]{2,1,0:T(8,128)S(1)}, u32[]{:S(2)}, u32[]{:S(2)}) collective-permute-start(f32[2,264,256]{2,1,0:T(8,128)S(1)} %pad_maximum_fusion.refs_0_.refs_5_), channel_id=1, source_target_pairs={{0,2},{1,3},{2,0},{3,1},{4,6},{5,7},{6,4},{7,5},{8,10},{9,11},{10,... | collective-permute-start | bytes 1622024 | tf_op jit(solution)/shard_map/ppermute | solution.py:38
  11.9 5.8 %copy-done = f32[2048,2048]{1,0:T(8,128)S(1)} copy-done((f32[2048,2048]{1,0:T(8,128)S(1)}, f32[2048,2048]{1,0:T(8,128)}, u32[]{:S(2)}) %copy-start) | copy-done | bytes 16777240
  17.6 3.1 %shard_map.84.refs_2_ = f32[512,2048]{1,0:T(8,128)S(1)} custom-call(s32[17]{0:T(128)S(1)} %stack.71.index, f32[2,264,256]{2,1,0:T(8,128)S(1)} %pad_maximum_fusion.refs_0_.refs_5_, f32[2048,2048]{1,0:T(8,128)S(1)} %copy-done), custom_call_target="tpu_custom_call" | custom-call | flops 1610612736 | bytes 1048576 | tf_op jit(solution)/shard_map/pallas_call | solution.py:54
  25.5 3.2 %shard_map.85.refs_4_ = f32[512,2048]{1,0:T(8,128)S(1)} custom-call(s32[17]{0:T(128)S(1)} %stack.71.index, f32[2,264,256]{2,1,0:T(8,128)S(1)} %collective-permute-done.refs_0_.refs_9_, f32[2048,2048]{1,0:T(8,128)S(1)} %copy-done, f32[512,2048]{1,0:T(8,128)S(1)} %shard_map.84.refs_2_), custom_call_target="tpu_custom_call" | custom-call | flops 1610612736 | bytes 1048576 | tf_op jit(solution)/shard_map/pallas_call | solution.py:54
  28.7 6.3 %collective-permute-done.2.refs_1_.refs_8_ = f32[2,264,256]{2,1,0:T(8,128)S(1)} collective-permute-done((f32[2,264,256]{2,1,0:T(8,128)S(1)}, f32[2,264,256]{2,1,0:T(8,128)S(1)}, u32[]{:S(2)}, u32[]{:S(2)}) %collective-permute-start.2) | collective-permute-done | bytes 540704 | tf_op jit(solution)/shard_map/ppermute | solution.py:38
  36.9 7.2 %shard_map.86.refs_4_ = f32[512,2048]{1,0:T(8,128)S(1)} custom-call(s32[17]{0:T(128)S(1)} %stack.71.index, f32[2,264,256]{2,1,0:T(8,128)} %collective-permute-done.1.refs_0_.refs_3_.refs_7_, f32[2,264,256]{2,1,0:T(8,128)S(1)} %copy-done.7, f32[2,264,256]{2,1,0:T(8,128)S(1)} %collective-permute-done.3.refs_2_.refs_6_, f32[2048,2048]{1,0:T(8,128)S(1)} %copy-done, ...), custom_call_target="tpu_custom_call" | custom-call | flops 4831838208 | bytes 1048576 | tf_op jit(solution)/shard_map/pallas_call | solution.py:54
  48.8 5.9 %shard_map.89 = (f32[512,1280]{1,0:T(8,128)S(1)}, bf16[512,1280]{1,0:T(8,128)(2,1)S(1)}, bf16[512,1280]{1,0:T(8,128)(2,1)S(1)}, f32[8,256]{1,0:T(8,128)S(1)}) custom-call(s32[17]{0:T(128)S(1)} %stack.71.index, f32[2,264,256]{2,1,0:T(8,128)S(1)} %collective-permute-done.6.refs_3_.refs_0_.refs_11_, f32[2,264,256]{2,1,0:T(8,128)S(1)} %collective-permute-done.4.refs_1_.refs_12_, ...), custom_call_target="tpu_custom_call" | custom-call | flops 3019898880 | bytes 1048576 | tf_op jit(solution)/shard_map/pallas_call | solution.py:54
  54.8 4.2 %shard_map.90 = (f32[512,768]{1,0:T(8,128)S(1)}, bf16[512,768]{1,0:T(8,128)(2,1)S(1)}, bf16[512,768]{1,0:T(8,128)(2,1)S(1)}, f32[8,256]{1,0:T(8,128)S(1)}) custom-call(s32[17]{0:T(128)S(1)} %stack.71.index, f32[2,264,256]{2,1,0:T(8,128)S(1)} %collective-permute-done.6.refs_3_.refs_0_.refs_11_, f32[2,264,256]{2,1,0:T(8,128)S(1)} %collective-permute-done.4.refs_1_.refs_12_, ...), custom_call_target="tpu_custom_call" | custom-call | flops 1811939328 | bytes 1048576 | tf_op jit(solution)/shard_map/pallas_call | solution.py:54
  67.0 4.1 %shard_map.92 = (f32[512,256]{1,0:T(8,128)S(1)}, f32[512,256]{1,0:T(8,128)S(1)}) custom-call(s32[17]{0:T(128)S(1)} %stack.71.index, f32[2048,2048]{1,0:T(8,128)S(1)} %bitcast.42, bf16[512,768]{1,0:T(8,128)(2,1)S(1)} %get-tuple-element.79.refs_0_.refs_4_, bf16[512,1280]{1,0:T(8,128)(2,1)S(1)} %get-tuple-element.80.refs_1_.refs_4_, ...), custom_call_target="tpu_custom_call" | custom-call | flops 3221225472 | bytes 1048576 | tf_op jit(solution)/shard_map/pallas_call | solution.py:54
  72.2 5.2 %collective-permute-start.16 = (f32[1]{0:T(128)}, f32[1]{0:T(128)}, u32[]{:S(2)}, u32[]{:S(2)}) collective-permute-start(f32[1]{0:T(128)} %add.330), channel_id=1, source_target_pairs={{0,64},{32,96},{64,0},{96,32},{1,65},{33,97},{65,1},{97,33},{2,66}... | collective-permute-start | bytes 20 | tf_op jit(solution)/shard_map/ppermute | solution.py:44
  80.2 3.7 %shard_map.93 = (f32[128,1280]{1,0:T(8,128)S(1)}, f32[128,1280]{1,0:T(8,128)S(1)}) custom-call(s32[17]{0:T(128)S(1)} %stack.71.index, bf16[8,128,512]{2,1,0:T(8,128)(2,1)S(1)} %get-tuple-element.85.refs_0_, bf16[8,128,512]{2,1,0:T(8,128)(2,1)S(1)} %get-tuple-element.86.refs_1_, bf16[8,128,512]{2,1,0:T(8,128)(2,1)S(1)} %get-tuple-element.77.refs_2_, ...), custom_call_target="tpu_custom_call" | custom-call | flops 2013265920 | bytes 1048576 | tf_op jit(solution)/shard_map/pallas_call | solution.py:54
  89.2 3.7 %shard_map.94 = f32[4,128,768]{2,1,0:T(8,128)S(1)} custom-call(s32[17]{0:T(128)S(1)} %stack.71.index, bf16[8,128,512]{2,1,0:T(8,128)(2,1)S(1)} %get-tuple-element.85.refs_0_, bf16[8,128,512]{2,1,0:T(8,128)(2,1)S(1)} %get-tuple-element.86.refs_1_, bf16[8,128,512]{2,1,0:T(8,128)(2,1)S(1)} %get-tuple-element.77.refs_2_, ...), custom_call_target="tpu_custom_call" | custom-call | flops 2415919104 | bytes 1048576 | tf_op jit(solution)/shard_map/pallas_call | solution.py:54
  92.9 3.7 %shard_map.95 = (f32[128,1280]{1,0:T(8,128)S(1)}, f32[128,1280]{1,0:T(8,128)S(1)}) custom-call(s32[17]{0:T(128)S(1)} %stack.71.index, bf16[8,128,512]{2,1,0:T(8,128)(2,1)S(1)} %get-tuple-element.85.refs_0_, bf16[8,128,512]{2,1,0:T(8,128)(2,1)S(1)} %get-tuple-element.86.refs_1_, bf16[8,128,512]{2,1,0:T(8,128)(2,1)S(1)} %get-tuple-element.77.refs_2_, ...), custom_call_target="tpu_custom_call" | custom-call | flops 2013265920 | bytes 1048576 | tf_op jit(solution)/shard_map/pallas_call | solution.py:54
  97.3 3.2 %collective-permute-start.18 = (f32[1]{0:T(128)}, f32[1]{0:T(128)}, u32[]{:S(2)}, u32[]{:S(2)}) collective-permute-start(f32[1]{0:T(128)} %add.332), channel_id=1, source_target_pairs={{0,4},{4,0},{1,5},{5,1},{2,6},{6,2},{3,7},{7,3},{8,12},{12,8},{9,1... | collective-permute-start | bytes 20 | tf_op jit(solution)/shard_map/ppermute | solution.py:44
  104.7 7.4 %shard_map.96 = (f32[2,512,256]{2,1,0:T(8,128)S(1)}, f32[2,512,256]{2,1,0:T(8,128)S(1)}) custom-call(s32[17]{0:T(128)S(1)} %stack.71.index, f32[2048,2048]{1,0:T(8,128)S(1)} %bitcast.42, bf16[512,768]{1,0:T(8,128)(2,1)S(1)} %get-tuple-element.79.refs_0_.refs_4_, bf16[512,1280]{1,0:T(8,128)(2,1)S(1)} %get-tuple-element.80.refs_1_.refs_4_, ...), custom_call_target="tpu_custom_call" | custom-call | flops 6442450944 | bytes 1048576 | tf_op jit(solution)/shard_map/pallas_call | solution.py:54
  112.4 3.1 %collective-permute-start.24 = (f32[2,512,256]{2,1,0:T(8,128)S(1)}, f32[2,512,256]{2,1,0:T(8,128)S(1)}, u32[]{:S(2)}, u32[]{:S(2)}) collective-permute-start(f32[2,512,256]{2,1,0:T(8,128)S(1)} %get-tuple-element.116), channel_id=1, source_target_pairs={{0,3},{1,0},{2,1},{3,2},{4,7},{5,4},{6,5},{7,6},{8,11},{9,8},{10,9... | collective-permute-start | bytes 3145736 | tf_op jit(solution)/shard_map/ppermute | solution.py:38
  115.4 5.7 %shard_map.97 = (f32[2,128,1280]{2,1,0:T(8,128)S(1)}, f32[2,128,1280]{2,1,0:T(8,128)S(1)}) custom-call(s32[17]{0:T(128)S(1)} %stack.71.index, bf16[8,128,512]{2,1,0:T(8,128)(2,1)S(1)} %get-tuple-element.85.refs_0_, bf16[8,128,512]{2,1,0:T(8,128)(2,1)S(1)} %get-tuple-element.86.refs_1_, bf16[8,128,512]{2,1,0:T(8,128)(2,1)S(1)} %get-tuple-element.77.refs_2_, ...), custom_call_target="tpu_custom_call" | custom-call | flops 4026531840 | bytes 1048576 | tf_op jit(solution)/shard_map/pallas_call | solution.py:54
  124.1 4.0 %shard_map.98 = (f32[512,256]{1,0:T(8,128)S(1)}, f32[512,256]{1,0:T(8,128)S(1)}) custom-call(s32[17]{0:T(128)S(1)} %stack.71.index, f32[2048,2048]{1,0:T(8,128)S(1)} %bitcast.42, bf16[512,768]{1,0:T(8,128)(2,1)S(1)} %get-tuple-element.79.refs_0_.refs_4_, bf16[512,1280]{1,0:T(8,128)(2,1)S(1)} %get-tuple-element.80.refs_1_.refs_4_, ...), custom_call_target="tpu_custom_call" | custom-call | flops 3221225472 | bytes 1048576 | tf_op jit(solution)/shard_map/pallas_call | solution.py:54
  128.8 5.2 %collective-permute-done.24 = f32[2,512,256]{2,1,0:T(8,128)S(1)} collective-permute-done((f32[2,512,256]{2,1,0:T(8,128)S(1)}, f32[2,512,256]{2,1,0:T(8,128)S(1)}, u32[]{:S(2)}, u32[]{:S(2)}) %collective-permute-start.24) | collective-permute-done | bytes 1048608 | tf_op jit(solution)/shard_map/ppermute | solution.py:38
  136.0 4.6 %shard_map.99 = (f32[128,768]{1,0:T(8,128)}, f32[128,768]{1,0:T(8,128)}, f32[128,768]{1,0:T(8,128)S(1)}, f32[128,768]{1,0:T(8,128)S(1)}) custom-call(s32[17]{0:T(128)S(1)} %stack.71.index, bf16[8,128,512]{2,1,0:T(8,128)(2,1)S(1)} %get-tuple-element.85.refs_0_, bf16[8,128,512]{2,1,0:T(8,128)(2,1)S(1)} %get-tuple-element.86.refs_1_, ...), custom_call_target="tpu_custom_call" | custom-call | flops 2415919104 | bytes 1048576 | tf_op jit(solution)/shard_map/pallas_call | solution.py:54
  146.9 2.9 %collective-permute-start.26 = (f32[1]{0:T(128)}, f32[1]{0:T(128)}, u32[]{:S(2)}, u32[]{:S(2)}) collective-permute-start(f32[1]{0:T(128)} %add.341), channel_id=1, source_target_pairs={{0,2},{1,3},{2,0},{3,1},{4,6},{5,7},{6,4},{7,5},{8,10},{9,11},{10,... | collective-permute-start | bytes 20 | tf_op jit(solution)/shard_map/ppermute | solution.py:44
  162.6 7.1 %collective-permute-done.27 = f32[128,768]{1,0:T(8,128)S(1)} collective-permute-done((f32[128,768]{1,0:T(8,128)}, f32[128,768]{1,0:T(8,128)S(1)}, u32[]{:S(2)}, u32[]{:S(2)}) %collective-permute-start.27) | collective-permute-done | bytes 393248 | tf_op jit(solution)/shard_map/ppermute | solution.py:38
  169.7 6.9 %collective-permute-done.28 = f32[128,768]{1,0:T(8,128)} collective-permute-done((f32[128,768]{1,0:T(8,128)}, f32[128,768]{1,0:T(8,128)}, u32[]{:S(2)}, u32[]{:S(2)}) %collective-permute-start.28) | collective-permute-done | bytes 393248 | tf_op jit(solution)/shard_map/ppermute | solution.py:38
  (113 shorter events, 63.4 us)
Async XLA Ops:
  3.3 17.4 %collective-permute-start = (f32[2,264,256]{2,1,0:T(8,128)S(1)}, f32[2,264,256]{2,1,0:T(8,128)S(1)}, u32[]{:S(2)}, u32[]{:S(2)}) collective-permute-start(f32[2,264,256]{2,1,0:T(8,128)S(1)} %pad_maximum_fusion.refs_0_.refs_5_), channel_id=1, source_target_pairs={{0,4},{4,0},{1,5},{5,1},{2,6},{6,2},{3,7},{7,3},{8,12},{12,8},{9,1... | collective-permute-start | bytes 1622024 | tf_op jit(solution)/shard_map/ppermute | solution.py:38
  6.7 17.3 %collective-permute-start.3 = (f32[2,264,256]{2,1,0:T(8,128)S(1)}, f32[2,264,256]{2,1,0:T(8,128)S(1)}, u32[]{:S(2)}, u32[]{:S(2)}) collective-permute-start(f32[2,264,256]{2,1,0:T(8,128)S(1)} %pad_maximum_fusion.refs_0_.refs_5_), channel_id=1, source_target_pairs={{0,2},{1,3},{2,0},{3,1},{4,6},{5,7},{6,4},{7,5},{8,10},{9,11},{10,... | collective-permute-start | bytes 1622024 | tf_op jit(solution)/shard_map/ppermute | solution.py:38
  9.7 25.3 %collective-permute-start.2 = (f32[2,264,256]{2,1,0:T(8,128)S(1)}, f32[2,264,256]{2,1,0:T(8,128)S(1)}, u32[]{:S(2)}, u32[]{:S(2)}) collective-permute-start(f32[2,264,256]{2,1,0:T(8,128)S(1)} %pad_maximum_fusion.refs_0_.refs_5_), channel_id=1, source_target_pairs={{0,3},{1,0},{2,1},{3,2},{4,7},{5,4},{6,5},{7,6},{8,11},{9,8},{10,9... | collective-permute-start | bytes 1622024 | tf_op jit(solution)/shard_map/ppermute | solution.py:38
  10.9 25.0 %collective-permute-start.1 = (f32[2,264,256]{2,1,0:T(8,128)S(1)}, f32[2,264,256]{2,1,0:T(8,128)}, u32[]{:S(2)}, u32[]{:S(2)}) collective-permute-start(f32[2,264,256]{2,1,0:T(8,128)S(1)} %pad_maximum_fusion.refs_0_.refs_5_), channel_id=1, source_target_pairs={{0,1},{1,2},{2,3},{3,0},{4,5},{5,6},{6,7},{7,4},{8,9},{9,10},{10,1... | collective-permute-start | bytes 1622024 | tf_op jit(solution)/shard_map/ppermute | solution.py:38
  20.7 24.9 %collective-permute-start.6 = (f32[2,264,256]{2,1,0:T(8,128)S(1)}, f32[2,264,256]{2,1,0:T(8,128)S(1)}, u32[]{:S(2)}, u32[]{:S(2)}) collective-permute-start(f32[2,264,256]{2,1,0:T(8,128)S(1)} %collective-permute-done.refs_0_.refs_9_), channel_id=1, source_target_pairs={{0,1},{1,2},{2,3},{3,0},{4,5},{5,6},{6,7},{7,4},{8,9},{9,10},{10,1... | collective-permute-start | bytes 1622024 | tf_op jit(solution)/shard_map/ppermute | solution.py:38
  21.4 24.2 %collective-permute-start.4 = (f32[2,264,256]{2,1,0:T(8,128)S(1)}, f32[2,264,256]{2,1,0:T(8,128)S(1)}, u32[]{:S(2)}, u32[]{:S(2)}) collective-permute-start(f32[2,264,256]{2,1,0:T(8,128)S(1)} %collective-permute-done.refs_0_.refs_9_), channel_id=1, source_target_pairs={{0,3},{1,0},{2,1},{3,2},{4,7},{5,4},{6,5},{7,6},{8,11},{9,8},{10,9... | collective-permute-start | bytes 1622024 | tf_op jit(solution)/shard_map/ppermute | solution.py:38
  24.0 21.5 %collective-permute-start.5 = (f32[2,264,256]{2,1,0:T(8,128)S(1)}, f32[2,264,256]{2,1,0:T(8,128)S(1)}, u32[]{:S(2)}, u32[]{:S(2)}) collective-permute-start(f32[2,264,256]{2,1,0:T(8,128)S(1)} %collective-permute-done.3.refs_2_.refs_6_), channel_id=1, source_target_pairs={{0,4},{4,0},{1,5},{5,1},{2,6},{6,2},{3,7},{7,3},{8,12},{12,8},{9,1... | collective-permute-start | bytes 1622024 | tf_op jit(solution)/shard_map/ppermute | solution.py:38
  54.8 25.4 %collective-permute-start.9 = (f32[512,1280]{1,0:T(8,128)S(1)}, f32[512,1280]{1,0:T(8,128)S(1)}, u32[]{:S(2)}, u32[]{:S(2)}) collective-permute-start(f32[512,1280]{1,0:T(8,128)S(1)} %get-tuple-element.73), channel_id=1, source_target_pairs={{0,8},{8,0},{1,9},{9,1},{2,10},{10,2},{3,11},{11,3},{4,12},{12,4},... | collective-permute-start | bytes 7864328 | tf_op jit(solution)/shard_map/ppermute | solution.py:38
  59.0 27.9 %collective-permute-start.10 = (f32[512,768]{1,0:T(8,128)S(1)}, f32[512,768]{1,0:T(8,128)S(1)}, u32[]{:S(2)}, u32[]{:S(2)}) collective-permute-start(f32[512,768]{1,0:T(8,128)S(1)} %get-tuple-element.75), channel_id=1, source_target_pairs={{0,8},{8,0},{1,9},{9,1},{2,10},{10,2},{3,11},{11,3},{4,12},{12,4},... | collective-permute-start | bytes 4718600 | tf_op jit(solution)/shard_map/ppermute | solution.py:38
  71.0 33.7 %collective-permute-start.11 = (f32[512,256]{1,0:T(8,128)S(1)}, f32[512,256]{1,0:T(8,128)S(1)}, u32[]{:S(2)}, u32[]{:S(2)}) collective-permute-start(f32[512,256]{1,0:T(8,128)S(1)} %get-tuple-element.83), channel_id=1, source_target_pairs={{0,1},{1,2},{2,3},{3,0},{4,5},{5,6},{6,7},{7,4},{8,9},{9,10},{10,1... | collective-permute-start | bytes 1572872 | tf_op jit(solution)/shard_map/ppermute | solution.py:38
  77.4 27.4 %collective-permute-start.12 = (f32[512,256]{1,0:T(8,128)S(1)}, f32[512,256]{1,0:T(8,128)S(1)}, u32[]{:S(2)}, u32[]{:S(2)}) collective-permute-start(f32[512,256]{1,0:T(8,128)S(1)} %get-tuple-element.93), channel_id=1, source_target_pairs={{0,3},{1,0},{2,1},{3,2},{4,7},{5,4},{6,5},{7,6},{8,11},{9,8},{10,9... | collective-permute-start | bytes 1572872 | tf_op jit(solution)/shard_map/ppermute | solution.py:38
  83.9 31.5 %collective-permute-start.13 = (f32[128,1280]{1,0:T(8,128)S(1)}, f32[128,1280]{1,0:T(8,128)S(1)}, u32[]{:S(2)}, u32[]{:S(2)}) collective-permute-start(f32[128,1280]{1,0:T(8,128)S(1)} %get-tuple-element.88), channel_id=1, source_target_pairs={{0,32},{32,64},{64,96},{96,0},{1,33},{33,65},{65,97},{97,1},{2,34}... | collective-permute-start | bytes 1966088 | tf_op jit(solution)/shard_map/ppermute | solution.py:38
  85.0 11.7 %collective-permute-start.17 = (f32[1]{0:T(128)}, f32[1]{0:T(128)}, u32[]{:S(2)}, u32[]{:S(2)}) collective-permute-start(f32[1]{0:T(128)} %add.331), channel_id=1, source_target_pairs={{0,16},{16,0},{1,17},{17,1},{2,18},{18,2},{3,19},{19,3},{4,20},{20... | collective-permute-start | bytes 20 | tf_op jit(solution)/shard_map/ppermute | solution.py:44
  87.0 28.4 %collective-permute-start.14 = (f32[128,1280]{1,0:T(8,128)S(1)}, f32[128,1280]{1,0:T(8,128)S(1)}, u32[]{:S(2)}, u32[]{:S(2)}) collective-permute-start(f32[128,1280]{1,0:T(8,128)S(1)} %get-tuple-element.96), channel_id=1, source_target_pairs={{0,96},{32,0},{64,32},{96,64},{1,97},{33,1},{65,33},{97,65},{2,98}... | collective-permute-start | bytes 1966088 | tf_op jit(solution)/shard_map/ppermute | solution.py:38
  103.1 33.0 %collective-permute-start.19 = (f32[4,128,768]{2,1,0:T(8,128)S(1)}, f32[4,128,768]{2,1,0:T(8,128)S(1)}, u32[]{:S(2)}, u32[]{:S(2)}) collective-permute-start(f32[4,128,768]{2,1,0:T(8,128)S(1)} %shard_map.94), channel_id=1, source_target_pairs={{0,16},{16,0},{1,17},{17,1},{2,18},{18,2},{3,19},{19,3},{4,20},{20... | collective-permute-start | bytes 4718600 | tf_op jit(solution)/shard_map/ppermute | solution.py:38
  112.1 22.6 %collective-permute-start.23 = (f32[2,512,256]{2,1,0:T(8,128)S(1)}, f32[2,512,256]{2,1,0:T(8,128)S(1)}, u32[]{:S(2)}, u32[]{:S(2)}) collective-permute-start(f32[2,512,256]{2,1,0:T(8,128)S(1)} %get-tuple-element.94), channel_id=1, source_target_pairs={{0,1},{1,2},{2,3},{3,0},{4,5},{5,6},{6,7},{7,4},{8,9},{9,10},{10,1... | collective-permute-start | bytes 3145736 | tf_op jit(solution)/shard_map/ppermute | solution.py:38
  112.4 21.6 %collective-permute-start.24 = (f32[2,512,256]{2,1,0:T(8,128)S(1)}, f32[2,512,256]{2,1,0:T(8,128)S(1)}, u32[]{:S(2)}, u32[]{:S(2)}) collective-permute-start(f32[2,512,256]{2,1,0:T(8,128)S(1)} %get-tuple-element.116), channel_id=1, source_target_pairs={{0,3},{1,0},{2,1},{3,2},{4,7},{5,4},{6,5},{7,6},{8,11},{9,8},{10,9... | collective-permute-start | bytes 3145736 | tf_op jit(solution)/shard_map/ppermute | solution.py:38
  122.1 31.2 %collective-permute-start.21 = (f32[2,128,1280]{2,1,0:T(8,128)S(1)}, f32[2,128,1280]{2,1,0:T(8,128)S(1)}, u32[]{:S(2)}, u32[]{:S(2)}) collective-permute-start(f32[2,128,1280]{2,1,0:T(8,128)S(1)} %get-tuple-element.112), channel_id=1, source_target_pairs={{0,96},{32,0},{64,32},{96,64},{1,97},{33,1},{65,33},{97,65},{2,98}... | collective-permute-start | bytes 3932168 | tf_op jit(solution)/shard_map/ppermute | solution.py:38
  122.7 32.1 %collective-permute-start.20 = (f32[2,128,1280]{2,1,0:T(8,128)S(1)}, f32[2,128,1280]{2,1,0:T(8,128)S(1)}, u32[]{:S(2)}, u32[]{:S(2)}) collective-permute-start(f32[2,128,1280]{2,1,0:T(8,128)S(1)} %get-tuple-element.97), channel_id=1, source_target_pairs={{0,32},{32,64},{64,96},{96,0},{1,33},{33,65},{65,97},{97,1},{2,34}... | collective-permute-start | bytes 3932168 | tf_op jit(solution)/shard_map/ppermute | solution.py:38
  140.6 19.7 %collective-permute-start.31 = (f32[512,256]{1,0:T(8,128)}, f32[512,256]{1,0:T(8,128)}, u32[]{:S(2)}, u32[]{:S(2)}) collective-permute-start(f32[512,256]{1,0:T(8,128)} %fusion.10), channel_id=1, source_target_pairs={{0,4},{4,0},{1,5},{5,1},{2,6},{6,2},{3,7},{7,3},{8,12},{12,8},{9,1... | collective-permute-start | bytes 1572872 | tf_op jit(solution)/shard_map/ppermute | solution.py:38
  155.9 13.7 %collective-permute-start.27 = (f32[128,768]{1,0:T(8,128)}, f32[128,768]{1,0:T(8,128)S(1)}, u32[]{:S(2)}, u32[]{:S(2)}) collective-permute-start(f32[128,768]{1,0:T(8,128)} %get-tuple-element.120), channel_id=1, source_target_pairs={{0,64},{32,96},{64,0},{96,32},{1,65},{33,97},{65,1},{97,33},{2,66}... | collective-permute-start | bytes 1179656 | tf_op jit(solution)/shard_map/ppermute | solution.py:38
  156.4 20.1 %collective-permute-start.28 = (f32[128,768]{1,0:T(8,128)}, f32[128,768]{1,0:T(8,128)}, u32[]{:S(2)}, u32[]{:S(2)}) collective-permute-start(f32[128,768]{1,0:T(8,128)} %get-tuple-element.121), channel_id=1, source_target_pairs={{0,32},{32,64},{64,96},{96,0},{1,33},{33,65},{65,97},{97,1},{2,34}... | collective-permute-start | bytes 1179656 | tf_op jit(solution)/shard_map/ppermute | solution.py:38
  157.1 19.4 %collective-permute-start.29 = (f32[128,768]{1,0:T(8,128)S(1)}, f32[128,768]{1,0:T(8,128)}, u32[]{:S(2)}, u32[]{:S(2)}) collective-permute-start(f32[128,768]{1,0:T(8,128)S(1)} %get-tuple-element.122), channel_id=1, source_target_pairs={{0,96},{32,0},{64,32},{96,64},{1,97},{33,1},{65,33},{97,65},{2,98}... | collective-permute-start | bytes 1179656 | tf_op jit(solution)/shard_map/ppermute | solution.py:38
  159.7 18.1 %collective-permute-start.30 = (f32[128,1280]{1,0:T(8,128)}, f32[128,1280]{1,0:T(8,128)}, u32[]{:S(2)}, u32[]{:S(2)}) collective-permute-start(f32[128,1280]{1,0:T(8,128)} %fusion.5), channel_id=1, source_target_pairs={{0,16},{16,0},{1,17},{17,1},{2,18},{18,2},{3,19},{19,3},{4,20},{20... | collective-permute-start | bytes 1966088 | tf_op jit(solution)/shard_map/ppermute | solution.py:38
  (30 other events, 255.3 us)

commit v3 on v2

--- a/solution.py
+++ b/solution.py
@@ -325,6 +325,19 @@
     )
 
 
+def update_body(index, zero, up, down, z_came, rest, y1, y2, y3, momentum, own, new_own, new_momentum):
+    for j in range(momentum.shape[1] // TN):
+        cols = pl.ds(j * TN, TN)
+        if j * TN < CY:
+            grad = (rest[:, cols] + y2[:, cols]) + (y1[:, cols] + y3[:, cols])
+        else:
+            here = pl.ds(j * TN - CY, TN)
+            grad = (zero[:, here] + (up[0, :, here] + down[0, :, here])) + z_came[:, here]
+        updated = momentum_rate * momentum[:, cols] + grad / TOKENS
+        new_momentum[:, cols] = updated
+        new_own[:, cols] = own[:, cols] - step_rate * updated
+
+
 def in_layer(teacher, student, gain, projector, momentum):
     _, cols = teacher.shape
     width = student.shape[1]
@@ -339,10 +352,12 @@
     left, right = shift(own, X, 1, 4), shift(own, X, -1, 4)
     far = shift(own, X, 2, 4)
     acc = forward(index, [own], at((0, 0)), projector)
-    acc = forward(after(index, acc), [upper], at((1, 0)), projector, acc)
     ul, ur = shift(upper, X, 1, 4), shift(upper, X, -1, 4)
+    acc = forward(
+        after(index, acc), [left, right, upper], at((0, 3), (0, 1), (1, 0)), projector, acc
+    )
     ufar = shift(far, YHI, 1, 2)
-    acc = forward(after(index, acc), [left, right, far], at((0, 3), (0, 1), (0, 2)), projector, acc)
+    acc = forward(after(index, acc), [far], at((0, 2)), projector, acc)
     hi, lo, sent_a = prepare(after(index, acc), [own, right, far, left], (0, 1, 2, 3))
     came_a = shift(sent_a, CORE, 1, 2)
     hi, lo, sent_b = prepare(after(index, sent_a), [upper, ur, ufar, ul], (4, 5, 6, 7), (hi, lo))
@@ -357,16 +372,20 @@
     res_y, *res_y_split, err_y = forward(after(index, res_z), *args, 0, CY // TN, 1)
     other_y = shift(res_y, CORE, 1, 2)
     error = jnp.sum(err_y + err_z).reshape(1)
-    error = sum_pair(error, Z)
+
+    def state(index, pairs, places, adds=()):
+        his, los = zip(res_y_split, res_z_split)
+        return state_blocks(index, at(*pairs), places, projector, his, los, adds)
+
+    apart = ((0, None), (1, None))
+    paired = ((0, 0), (0, 1), (1, 0), (1, 1))
+    sfar = state(after(index, res_y), ((0, 2), (1, 2)), apart)
+    sfo, sft = shift(sfar[0], X, 1, 4), shift(sfar[1], X, -1, 4)
     splits = (
         hi,
         lo,
-        *turned(after(index, res_y), (came_a, came_b), ((0, 1, 2, 3), (4, 5, 6, 7))),
-    )
-
-    def state(index, pairs, places, adds=()):
-        his, los = zip(res_y_split, res_z_split)
-        return state_blocks(index, at(*pairs), places, projector, his, los, adds)
+        *turned(after(index, sfar[0]), (came_a, came_b), ((0, 1, 2, 3), (4, 5, 6, 7))),
+    )
 
     def grad_y(index, pairs, places, adds=()):
         slots = [SLOT[p] for p in pairs]
@@ -376,23 +395,14 @@
         slots = [SLOT[p] for p in pairs]
         return grad_blocks(index, slots, places, splits, res_z_split, other_z, adds)
 
-    apart = ((0, None), (1, None))
-    paired = ((0, 0), (0, 1), (1, 0), (1, 1))
-    sfar = state(after(index, splits[2]), ((0, 2), (1, 2)), apart)
-    sfo, sft = shift(sfar[0], X, 1, 4), shift(sfar[1], X, -1, 4)
-    error = sum_pair(after(error, sfar[0]), Z, far=True)
-    zfar = grad_z(after(index, sfar[0]), ((2, 0), (2, 1)), apart)
+    zfar = grad_z(after(index, splits[2]), ((2, 0), (2, 1)), apart)
     zfo, zft = shift(zfar[0], Z, 1, 4), shift(zfar[1], Z, -1, 4)
-    error = sum_pair(after(error, zfar[0]), YLO)
     (ys,) = grad_y(
         after(index, zfar[0]), ((2, 1), (1, 1), (3, 1), (0, 1)), ((0, 0), (0, 1), (0, 2), (0, 3))
     )
-    error = sum_pair(after(error, ys), YHI)
-    zero = grad_z(after(index, ys), ((0, 0), (0, 1)), apart)
-    ys, error, _ = lax.optimization_barrier((ys, error, zero[0]))
-    ys = shift(ys, YLO, 1, 2)
+    ys_came = shift(ys, YLO, 1, 2)
     sup, sdown = state(
-        after(index, zero[0]), ((0, 1), (1, 1), (0, 3), (1, 3)), paired, ((0, sfo), (3, sft))
+        after(index, ys), ((0, 1), (1, 1), (0, 3), (1, 3)), paired, ((0, sfo), (3, sft))
     )
     sup_came, sdown_came = shift(sup, X, 1, 4), shift(sdown, X, -1, 4)
     up, down = grad_z(
@@ -404,33 +414,40 @@
     up_came, down_came = shift(up, Z, 1, 4), shift(down, Z, -1, 4)
     error = sum_pair(after(error, up), CORE)
     s0 = state(after(index, up), ((0, 0), (1, 0)), apart)
+    zero = grad_z(after(index, s0[0]), ((0, 0), (0, 1)), apart)
+    error = sum_pair(after(error, zero[0]), YLO)
     two, one, three, rest = grad_y(
-        after(index, s0[0]),
+        after(index, zero[0]),
         ((2, 0), (1, 0), (3, 0), (0, 0)),
         ((0, None), (1, None), (2, None), (3, None)),
-        tuple((k, k, ys) for k in range(4)),
-    )
+        tuple((k, k, ys_came) for k in range(4)),
+    )
+    error = sum_pair(after(error, rest), YHI)
     s_part = s0[1] + (sup_came[1] + sdown_came[1])
     s_part, _ = lax.optimization_barrier((s_part, rest))
     s_came = shift(s_part, YHI, 1, 2)
-    error = sum_pair(after(error, s_part), X)
-    error = sum_pair(error, X, far=True)
+    error = sum_pair(after(error, up_came, down_came), Z)
     z_part = zero[1] + (up_came[1] + down_came[1])
-    z_part, error, _ = lax.optimization_barrier((z_part, error, s_part))
+    z_part, _ = lax.optimization_barrier((z_part, s_part))
     two, one, three, _ = lax.optimization_barrier((two, one, three, z_part))
+    z_came = shift(z_part, YLO, 1, 2)
     y2 = shift(two, Z, 2, 4)
     y1, y3 = shift(one, Z, 1, 4), shift(three, Z, -1, 4)
-    z_came = shift(z_part, YLO, 1, 2)
-    grad_hi = (zero[0] + (up_came[0] + down_came[0])) + z_came
-    grad_lo = (rest + y2) + (y1 + y3)
-    proj_grad = jnp.concatenate([grad_lo, grad_hi], 1) / TOKENS
     student_grad = (s0[0] + (sup_came[0] + sdown_came[0])) + s_came
+    error = sum_pair(after(error, z_part, student_grad), X)
+    error = sum_pair(error, X, far=True)
+    error = sum_pair(after(error, y1, y2, y3), Z, far=True)
     loss_value = error[0] / (TOKENS * DT)
 
-    new_momentum = momentum_rate * momentum + proj_grad
     own_block = lax.axis_index(Z) * 4 + lax.axis_index(YLO) * 2 + lax.axis_index(CORE)
     own_rows = lax.dynamic_slice_in_dim(projector, own_block * half, half, 0)
-    new_projector = own_rows - step_rate * new_momentum
+    new_projector, new_momentum = kernel(
+        update_body,
+        index,
+        [zero[0], up_came, down_came, z_came, rest, y1, y2, y3, momentum, own_rows],
+        [of(momentum.shape)] * 2,
+        MIB,
+    )
     return (new_projector, new_momentum, student_grad, loss_value)
 
 

time: 185 us -> 192 us (1.038)
  waiting for transfers between devices: 36.7 us -> 22.6 us
  starting transfers between devices: 52.1 us -> 63.7 us
  local copies, waits for them, and re-layouts: 10 us -> 20.8 us
  other arithmetic: 13 us -> 8.21 us
  Pallas kernels: 64.1 us -> 68.7 us
    ppermute x25, waiting for transfers between devices: 28.7 us -> 12.9 us  [shift(): lax.ppermute(value, axis, [(i, (i + by) % size) for i in range(size)])]
    ppermute x7, starting transfers between devices: 17.7 us -> 27.3 us  [sum_pair(): lax.ppermute(value, axis, [(i, i ^ step) for i in range(size)])]
    unnamed x44 -> x60, local copies, waits for them, and re-layouts: 9.93 us -> 19.4 us
    pallas_call x16 -> x17, Pallas kernels: 64.1 us -> 68.7 us  [kernel(): pl.pallas_call(body, in_specs=specs, out_specs=[pl.BlockSpec(memory_space...]
    sub x1 -> x0, other arithmetic: 2.84 us -> none  [in_layer(): new_projector = own_rows - step_rate * new_momentum]
    add x2 -> x0, other arithmetic: 2.56 us -> none  [the longest x1 1.34 us: in_layer(): grad_hi = zero[0] + (up_came[0] + down_came[0]) + z_came]
    ppermute x25, starting transfers between devices: 34.4 us -> 36.5 us  [shift(): lax.ppermute(value, axis, [(i, (i + by) % size) for i in range(size)])]
  transfers between devices with their start and end apart: 32 -> 32, of which waited for: 12 -> 9; matrix products, arithmetic and copies ran while one was open for 3% -> 4% of each run, Pallas kernels for 31% -> 31%
where the time goes in v3:
time: 192 us; the launch traced here: 191 us
  Pallas kernels  68.7 us (36%)
  starting transfers between devices  63.7 us (33%)
  waiting for transfers between devices  22.6 us (12%)
  local copies, waits for them, and re-layouts  20.8 us (11%)
  other arithmetic  8.21 us (4%)
  between operations  7.17 us (4%)
    pallas_call x17, Pallas kernels, kernel(): pl.pallas_call(body, in_specs=specs, out_specs=[pl.BlockSpec(memory_space...  68.7 us
    ppermute x25, starting transfers between devices, shift(): lax.ppermute(value, axis, [(i, (i + by) % size) for i in range(size)])  36.5 us
    ppermute x7, starting transfers between devices, sum_pair(): lax.ppermute(value, axis, [(i, i ^ step) for i in range(size)])  27.3 us
    unnamed x60, local copies, waits for them, and re-layouts  19.4 us
    ppermute x25, waiting for transfers between devices, shift(): lax.ppermute(value, axis, [(i, (i + by) % size) for i in range(size)])  12.9 us
    ppermute x7, waiting for transfers between devices, sum_pair(): lax.ppermute(value, axis, [(i, i ^ step) for i in range(size)])  9.6 us
  transfers between devices with their start and end apart: 32, of which 9 were waited for; matrix products, arithmetic and copies ran while one was open for 4% of the time, Pallas kernels for 31%

profile of v3, /device:TPU:0, one launch (start us, length us, event | category | flops | bytes accessed | tf_op | source)
XLA Modules:
  0.0 191.1 jit_solution(16652362872808726290)
XLA Ops:
  3.3 3.4 %collective-permute-start.2 = (f32[2,264,256]{2,1,0:T(8,128)S(1)}, f32[2,264,256]{2,1,0:T(8,128)S(1)}, u32[]{:S(2)}, u32[]{:S(2)}) collective-permute-start(f32[2,264,256]{2,1,0:T(8,128)S(1)} %pad_maximum_fusion.refs_0_.refs_5_), channel_id=1, source_target_pairs={{0,4},{4,0},{1,5},{5,1},{2,6},{6,2},{3,7},{7,3},{8,12},{12,8},{9,1... | collective-permute-start | bytes 1622024 | tf_op jit(solution)/shard_map/ppermute | solution.py:38
  6.7 3.0 %collective-permute-start.3 = (f32[2,264,256]{2,1,0:T(8,128)S(1)}, f32[2,264,256]{2,1,0:T(8,128)S(1)}, u32[]{:S(2)}, u32[]{:S(2)}) collective-permute-start(f32[2,264,256]{2,1,0:T(8,128)S(1)} %pad_maximum_fusion.refs_0_.refs_5_), channel_id=1, source_target_pairs={{0,2},{1,3},{2,0},{3,1},{4,6},{5,7},{6,4},{7,5},{8,10},{9,11},{10,... | collective-permute-start | bytes 1622024 | tf_op jit(solution)/shard_map/ppermute | solution.py:38
  13.1 5.8 %copy-done = f32[2048,2048]{1,0:T(8,128)S(1)} copy-done((f32[2048,2048]{1,0:T(8,128)S(1)}, f32[2048,2048]{1,0:T(8,128)}, u32[]{:S(2)}) %copy-start) | copy-done | bytes 16777240
  18.8 3.1 %shard_map.84.refs_4_ = f32[512,2048]{1,0:T(8,128)S(1)} custom-call(s32[17]{0:T(128)S(1)} %stack.71.index, f32[2,264,256]{2,1,0:T(8,128)S(1)} %pad_maximum_fusion.refs_0_.refs_5_, f32[2048,2048]{1,0:T(8,128)S(1)} %copy-done), custom_call_target="tpu_custom_call" | custom-call | flops 1610612736 | bytes 1048576 | tf_op jit(solution)/shard_map/pallas_call | solution.py:54
  25.0 9.0 %collective-permute-done.refs_0_.refs_3_.refs_7_ = f32[2,264,256]{2,1,0:T(8,128)S(1)} collective-permute-done((f32[2,264,256]{2,1,0:T(8,128)S(1)}, f32[2,264,256]{2,1,0:T(8,128)S(1)}, u32[]{:S(2)}, u32[]{:S(2)}) %collective-permute-start) | collective-permute-done | bytes 540704 | tf_op jit(solution)/shard_map/ppermute | solution.py:38
  35.1 6.8 %shard_map.85.refs_2_ = f32[512,2048]{1,0:T(8,128)S(1)} custom-call(s32[17]{0:T(128)S(1)} %stack.71.index, f32[2,264,256]{2,1,0:T(8,128)S(1)} %collective-permute-done.refs_0_.refs_3_.refs_7_, f32[2,264,256]{2,1,0:T(8,128)S(1)} %collective-permute-done.1.refs_1_.refs_8_, f32[2,264,256]{2,1,0:T(8,128)S(1)} %collective-permute-done.2.refs_2_.refs_0_.refs_9_, ...), custom_call_target="tpu_custom_call" | custom-call | flops 4831838208 | bytes 1048576 | tf_op jit(solution)/shard_map/pallas_call | solution.py:54
  41.9 3.3 %shard_map.86.refs_4_ = f32[512,2048]{1,0:T(8,128)S(1)} custom-call(s32[17]{0:T(128)S(1)} %stack.71.index, f32[2,264,256]{2,1,0:T(8,128)S(1)} %collective-permute-done.3.refs_0_.refs_2_.refs_6_, f32[2048,2048]{1,0:T(8,128)S(1)} %copy-done.1, f32[512,2048]{1,0:T(8,128)S(1)} %shard_map.85.refs_2_), custom_call_target="tpu_custom_call" | custom-call | flops 1610612736 | bytes 1048576 | tf_op jit(solution)/shard_map/pallas_call | solution.py:54
  51.1 5.4 %shard_map.89 = (f32[512,1280]{1,0:T(8,128)S(1)}, bf16[512,1280]{1,0:T(8,128)(2,1)S(1)}, bf16[512,1280]{1,0:T(8,128)(2,1)S(1)}, f32[8,256]{1,0:T(8,128)S(1)}) custom-call(s32[17]{0:T(128)S(1)} %stack.71.index, f32[2,264,256]{2,1,0:T(8,128)S(1)} %collective-permute-done.6.refs_3_.refs_0_.refs_11_, f32[2,264,256]{2,1,0:T(8,128)S(1)} %collective-permute-done.4.refs_1_.refs_12_, ...), custom_call_target="tpu_custom_call" | custom-call | flops 3019898880 | bytes 1048576 | tf_op jit(solution)/shard_map/pallas_call | solution.py:54
  56.6 3.7 %shard_map.90 = (f32[512,768]{1,0:T(8,128)S(1)}, bf16[512,768]{1,0:T(8,128)(2,1)S(1)}, bf16[512,768]{1,0:T(8,128)(2,1)S(1)}, f32[8,256]{1,0:T(8,128)S(1)}) custom-call(s32[17]{0:T(128)S(1)} %stack.71.index, f32[2,264,256]{2,1,0:T(8,128)S(1)} %collective-permute-done.6.refs_3_.refs_0_.refs_11_, f32[2,264,256]{2,1,0:T(8,128)S(1)} %collective-permute-done.4.refs_1_.refs_12_, ...), custom_call_target="tpu_custom_call" | custom-call | flops 1811939328 | bytes 1048576 | tf_op jit(solution)/shard_map/pallas_call | solution.py:54
  61.4 4.1 %shard_map.91 = (f32[512,256]{1,0:T(8,128)S(1)}, f32[512,256]{1,0:T(8,128)S(1)}) custom-call(s32[17]{0:T(128)S(1)} %stack.71.index, f32[2048,2048]{1,0:T(8,128)S(1)} %copy-done.1, bf16[512,768]{1,0:T(8,128)(2,1)S(1)} %get-tuple-element.77.refs_0_.refs_4_, bf16[512,1280]{1,0:T(8,128)(2,1)S(1)} %get-tuple-element.78.refs_1_.refs_4_, ...), custom_call_target="tpu_custom_call" | custom-call | flops 3221225472 | bytes 1048576 | tf_op jit(solution)/shard_map/pallas_call | solution.py:54
  70.0 3.7 %shard_map.93 = (f32[128,1280]{1,0:T(8,128)S(1)}, f32[128,1280]{1,0:T(8,128)S(1)}) custom-call(s32[17]{0:T(128)S(1)} %stack.71.index, bf16[8,128,512]{2,1,0:T(8,128)(2,1)S(1)} %get-tuple-element.85.refs_0_, bf16[8,128,512]{2,1,0:T(8,128)(2,1)S(1)} %get-tuple-element.86.refs_1_, bf16[8,128,512]{2,1,0:T(8,128)(2,1)S(1)} %get-tuple-element.83.refs_2_, ...), custom_call_target="tpu_custom_call" | custom-call | flops 2013265920 | bytes 1048576 | tf_op jit(solution)/shard_map/pallas_call | solution.py:54
  77.9 4.9 %shard_map.94 = f32[4,128,768]{2,1,0:T(8,128)} custom-call(s32[17]{0:T(128)S(1)} %stack.71.index, bf16[8,128,512]{2,1,0:T(8,128)(2,1)S(1)} %get-tuple-element.85.refs_0_, bf16[8,128,512]{2,1,0:T(8,128)(2,1)S(1)} %get-tuple-element.86.refs_1_, bf16[8,128,512]{2,1,0:T(8,128)(2,1)S(1)} %get-tuple-element.83.refs_2_, ...), custom_call_target="tpu_custom_call" | custom-call | flops 2415919104 | bytes 1048576 | tf_op jit(solution)/shard_map/pallas_call | solution.py:54
  83.5 8.5 %shard_map.95 = (f32[2,512,256]{2,1,0:T(8,128)}, f32[2,512,256]{2,1,0:T(8,128)}) custom-call(s32[17]{0:T(128)S(1)} %stack.71.index, f32[2048,2048]{1,0:T(8,128)S(1)} %copy-done.1, bf16[512,768]{1,0:T(8,128)(2,1)S(1)} %get-tuple-element.77.refs_0_.refs_4_, bf16[512,1280]{1,0:T(8,128)(2,1)S(1)} %get-tuple-element.78.refs_1_.refs_4_, ...), custom_call_target="tpu_custom_call" | custom-call | flops 6442450944 | bytes 1048576 | tf_op jit(solution)/shard_map/pallas_call | solution.py:54
  92.2 3.0 %collective-permute-start.18 = (f32[2,512,256]{2,1,0:T(8,128)}, f32[2,512,256]{2,1,0:T(8,128)}, u32[]{:S(2)}, u32[]{:S(2)}) collective-permute-start(f32[2,512,256]{2,1,0:T(8,128)} %get-tuple-element.103), channel_id=1, source_target_pairs={{0,3},{1,0},{2,1},{3,2},{4,7},{5,4},{6,5},{7,6},{8,11},{9,8},{10,9... | collective-permute-start | bytes 3145736 | tf_op jit(solution)/shard_map/ppermute | solution.py:38
  95.3 7.3 %shard_map.96 = (f32[2,128,1280]{2,1,0:T(8,128)}, f32[2,128,1280]{2,1,0:T(8,128)}) custom-call(s32[17]{0:T(128)S(1)} %stack.71.index, bf16[8,128,512]{2,1,0:T(8,128)(2,1)S(1)} %get-tuple-element.85.refs_0_, bf16[8,128,512]{2,1,0:T(8,128)(2,1)S(1)} %get-tuple-element.86.refs_1_, bf16[8,128,512]{2,1,0:T(8,128)(2,1)S(1)} %get-tuple-element.83.refs_2_, ...), custom_call_target="tpu_custom_call" | custom-call | flops 4026531840 | bytes 1048576 | tf_op jit(solution)/shard_map/pallas_call | solution.py:54
  102.6 3.2 %collective-permute-start.16 = (f32[2,128,1280]{2,1,0:T(8,128)}, f32[2,128,1280]{2,1,0:T(8,128)}, u32[]{:S(2)}, u32[]{:S(2)}) collective-permute-start(f32[2,128,1280]{2,1,0:T(8,128)} %get-tuple-element.100), channel_id=1, source_target_pairs={{0,96},{32,0},{64,32},{96,64},{1,97},{33,1},{65,33},{97,65},{2,98}... | collective-permute-start | bytes 3932168 | tf_op jit(solution)/shard_map/ppermute | solution.py:38
  105.8 5.8 %copy-done.2 = f32[2048,2048]{1,0:T(8,128)S(1)} copy-done((f32[2048,2048]{1,0:T(8,128)S(1)}, f32[2048,2048]{1,0:T(8,128)}, u32[]{:S(2)}) %copy-start.2) | copy-done | bytes 16777240
  115.2 4.1 %shard_map.97 = (f32[512,256]{1,0:T(8,128)S(1)}, f32[512,256]{1,0:T(8,128)S(1)}) custom-call(s32[17]{0:T(128)S(1)} %stack.71.index, f32[2048,2048]{1,0:T(8,128)S(1)} %copy-done.2, bf16[512,768]{1,0:T(8,128)(2,1)S(1)} %copy-done.22, bf16[512,1280]{1,0:T(8,128)(2,1)S(1)} %get-tuple-element.78.refs_1_.refs_4_, bf16[512,768]{1,0:T(8,128)(2,1)S(1)} %copy-done.24, ...), custom_call_target="tpu_custom_call" | custom-call | flops 3221225472 | bytes 1048576 | tf_op jit(solution)/shard_map/pallas_call | solution.py:54
  119.3 3.7 %shard_map.98 = (f32[128,1280]{1,0:T(8,128)S(1)}, f32[128,1280]{1,0:T(8,128)S(1)}) custom-call(s32[17]{0:T(128)S(1)} %stack.71.index, bf16[8,128,512]{2,1,0:T(8,128)(2,1)S(1)} %copy-done.9, bf16[8,128,512]{2,1,0:T(8,128)(2,1)S(1)} %copy-done.11, bf16[8,128,512]{2,1,0:T(8,128)(2,1)S(1)} %copy-done.13, bf16[8,128,512]{2,1,0:T(8,128)(2,1)S(1)} %copy-done.15, ...), custom_call_target="tpu_custom_call" | custom-call | flops 2013265920 | bytes 1048576 | tf_op jit(solution)/shard_map/pallas_call | solution.py:54
  124.7 3.7 %shard_map.99 = (f32[128,768]{1,0:T(8,128)S(1)}, f32[128,768]{1,0:T(8,128)S(1)}, f32[128,768]{1,0:T(8,128)S(1)}, f32[128,768]{1,0:T(8,128)S(1)}) custom-call(s32[17]{0:T(128)S(1)} %stack.71.index, bf16[8,128,512]{2,1,0:T(8,128)(2,1)S(1)} %copy-done.9, bf16[8,128,512]{2,1,0:T(8,128)(2,1)S(1)} %copy-done.11, bf16[8,128,512]{2,1,0:T(8,128)(2,1)S(1)} %copy-done.13, ...), custom_call_target="tpu_custom_call" | custom-call | flops 2415919104 | bytes 1048576 | tf_op jit(solution)/shard_map/pallas_call | solution.py:54
  139.3 14.4 %collective-permute-start.26 = (f32[1]{0:T(128)}, f32[1]{0:T(128)}, u32[]{:S(2)}, u32[]{:S(2)}) collective-permute-start(f32[1]{0:T(128)} %add.316), channel_id=1, source_target_pairs={{0,16},{16,0},{1,17},{17,1},{2,18},{18,2},{3,19},{19,3},{4,20},{20... | collective-permute-start | bytes 20 | tf_op jit(solution)/shard_map/ppermute | solution.py:44
  154.6 5.2 %collective-permute-start.27 = (f32[1]{0:T(128)}, f32[1]{0:T(128)}, u32[]{:S(2)}, u32[]{:S(2)}) collective-permute-start(f32[1]{0:T(128)} %add.317), channel_id=1, source_target_pairs={{0,4},{4,0},{1,5},{5,1},{2,6},{6,2},{3,7},{7,3},{8,12},{12,8},{9,1... | collective-permute-start | bytes 20 | tf_op jit(solution)/shard_map/ppermute | solution.py:44
  177.2 2.9 %collective-permute-done.30 = f32[1]{0:T(128)} collective-permute-done((f32[1]{0:T(128)}, f32[1]{0:T(128)}, u32[]{:S(2)}, u32[]{:S(2)}) %collective-permute-start.30) | collective-permute-done | bytes 36 | tf_op jit(solution)/shard_map/ppermute | solution.py:44
  186.6 3.4 %shard_map.100 = (f32[128,2048]{1,0:T(8,128)}, f32[128,2048]{1,0:T(8,128)}) custom-call(s32[17]{0:T(128)S(1)} %stack.71.index, f32[128,1280]{1,0:T(8,128)S(1)} %get-tuple-element.99.zero, f32[2,128,1280]{2,1,0:T(8,128)} %collective-permute-done.15.up, f32[2,128,1280]{2,1,0:T(8,128)} %collective-permute-done.16.down, ...), custom_call_target="tpu_custom_call" | custom-call | flops 1048576 | bytes 1048576 | tf_op jit(solution)/shard_map/pallas_call | solution.py:54
  (127 shorter events, 62.6 us)
Async XLA Ops:
  3.3 18.6 %collective-permute-start.2 = (f32[2,264,256]{2,1,0:T(8,128)S(1)}, f32[2,264,256]{2,1,0:T(8,128)S(1)}, u32[]{:S(2)}, u32[]{:S(2)}) collective-permute-start(f32[2,264,256]{2,1,0:T(8,128)S(1)} %pad_maximum_fusion.refs_0_.refs_5_), channel_id=1, source_target_pairs={{0,4},{4,0},{1,5},{5,1},{2,6},{6,2},{3,7},{7,3},{8,12},{12,8},{9,1... | collective-permute-start | bytes 1622024 | tf_op jit(solution)/shard_map/ppermute | solution.py:38
  6.7 17.4 %collective-permute-start.3 = (f32[2,264,256]{2,1,0:T(8,128)S(1)}, f32[2,264,256]{2,1,0:T(8,128)S(1)}, u32[]{:S(2)}, u32[]{:S(2)}) collective-permute-start(f32[2,264,256]{2,1,0:T(8,128)S(1)} %pad_maximum_fusion.refs_0_.refs_5_), channel_id=1, source_target_pairs={{0,2},{1,3},{2,0},{3,1},{4,6},{5,7},{6,4},{7,5},{8,10},{9,11},{10,... | collective-permute-start | bytes 1622024 | tf_op jit(solution)/shard_map/ppermute | solution.py:38
  9.7 24.3 %collective-permute-start = (f32[2,264,256]{2,1,0:T(8,128)S(1)}, f32[2,264,256]{2,1,0:T(8,128)S(1)}, u32[]{:S(2)}, u32[]{:S(2)}) collective-permute-start(f32[2,264,256]{2,1,0:T(8,128)S(1)} %pad_maximum_fusion.refs_0_.refs_5_), channel_id=1, source_target_pairs={{0,1},{1,2},{2,3},{3,0},{4,5},{5,6},{6,7},{7,4},{8,9},{9,10},{10,1... | collective-permute-start | bytes 1622024 | tf_op jit(solution)/shard_map/ppermute | solution.py:38
  10.3 24.7 %collective-permute-start.1 = (f32[2,264,256]{2,1,0:T(8,128)S(1)}, f32[2,264,256]{2,1,0:T(8,128)S(1)}, u32[]{:S(2)}, u32[]{:S(2)}) collective-permute-start(f32[2,264,256]{2,1,0:T(8,128)S(1)} %pad_maximum_fusion.refs_0_.refs_5_), channel_id=1, source_target_pairs={{0,3},{1,0},{2,1},{3,2},{4,7},{5,4},{6,5},{7,6},{8,11},{9,8},{10,9... | collective-permute-start | bytes 1622024 | tf_op jit(solution)/shard_map/ppermute | solution.py:38
  22.0 24.2 %collective-permute-start.4 = (f32[2,264,256]{2,1,0:T(8,128)S(1)}, f32[2,264,256]{2,1,0:T(8,128)S(1)}, u32[]{:S(2)}, u32[]{:S(2)}) collective-permute-start(f32[2,264,256]{2,1,0:T(8,128)S(1)} %collective-permute-done.2.refs_2_.refs_0_.refs_9_), channel_id=1, source_target_pairs={{0,3},{1,0},{2,1},{3,2},{4,7},{5,4},{6,5},{7,6},{8,11},{9,8},{10,9... | collective-permute-start | bytes 1622024 | tf_op jit(solution)/shard_map/ppermute | solution.py:38
  22.0 24.1 %collective-permute-start.6 = (f32[2,264,256]{2,1,0:T(8,128)S(1)}, f32[2,264,256]{2,1,0:T(8,128)S(1)}, u32[]{:S(2)}, u32[]{:S(2)}) collective-permute-start(f32[2,264,256]{2,1,0:T(8,128)S(1)} %collective-permute-done.2.refs_2_.refs_0_.refs_9_), channel_id=1, source_target_pairs={{0,1},{1,2},{2,3},{3,0},{4,5},{5,6},{6,7},{7,4},{8,9},{9,10},{10,1... | collective-permute-start | bytes 1622024 | tf_op jit(solution)/shard_map/ppermute | solution.py:38
  24.1 22.1 %collective-permute-start.5 = (f32[2,264,256]{2,1,0:T(8,128)S(1)}, f32[2,264,256]{2,1,0:T(8,128)S(1)}, u32[]{:S(2)}, u32[]{:S(2)}) collective-permute-start(f32[2,264,256]{2,1,0:T(8,128)S(1)} %collective-permute-done.3.refs_0_.refs_2_.refs_6_), channel_id=1, source_target_pairs={{0,4},{4,0},{1,5},{5,1},{2,6},{6,2},{3,7},{7,3},{8,12},{12,8},{9,1... | collective-permute-start | bytes 1622024 | tf_op jit(solution)/shard_map/ppermute | solution.py:38
  56.5 13.5 %collective-permute-start.9 = (f32[512,1280]{1,0:T(8,128)S(1)}, f32[512,1280]{1,0:T(8,128)S(1)}, u32[]{:S(2)}, u32[]{:S(2)}) collective-permute-start(f32[512,1280]{1,0:T(8,128)S(1)} %get-tuple-element.73), channel_id=1, source_target_pairs={{0,8},{8,0},{1,9},{9,1},{2,10},{10,2},{3,11},{11,3},{4,12},{12,4},... | collective-permute-start | bytes 7864328 | tf_op jit(solution)/shard_map/ppermute | solution.py:38
  60.3 17.6 %collective-permute-start.10 = (f32[512,768]{1,0:T(8,128)S(1)}, f32[512,768]{1,0:T(8,128)S(1)}, u32[]{:S(2)}, u32[]{:S(2)}) collective-permute-start(f32[512,768]{1,0:T(8,128)S(1)} %get-tuple-element.75), channel_id=1, source_target_pairs={{0,8},{8,0},{1,9},{9,1},{2,10},{10,2},{3,11},{11,3},{4,12},{12,4},... | collective-permute-start | bytes 4718600 | tf_op jit(solution)/shard_map/ppermute | solution.py:38
  65.5 18.0 %collective-permute-start.11 = (f32[512,256]{1,0:T(8,128)S(1)}, f32[512,256]{1,0:T(8,128)S(1)}, u32[]{:S(2)}, u32[]{:S(2)}) collective-permute-start(f32[512,256]{1,0:T(8,128)S(1)} %get-tuple-element.81), channel_id=1, source_target_pairs={{0,1},{1,2},{2,3},{3,0},{4,5},{5,6},{6,7},{7,4},{8,9},{9,10},{10,1... | collective-permute-start | bytes 1572872 | tf_op jit(solution)/shard_map/ppermute | solution.py:38
  67.0 16.5 %collective-permute-start.12 = (f32[512,256]{1,0:T(8,128)S(1)}, f32[512,256]{1,0:T(8,128)S(1)}, u32[]{:S(2)}, u32[]{:S(2)}) collective-permute-start(f32[512,256]{1,0:T(8,128)S(1)} %get-tuple-element.91), channel_id=1, source_target_pairs={{0,3},{1,0},{2,1},{3,2},{4,7},{5,4},{6,5},{7,6},{8,11},{9,8},{10,9... | collective-permute-start | bytes 1572872 | tf_op jit(solution)/shard_map/ppermute | solution.py:38
  73.7 21.6 %collective-permute-start.13 = (f32[128,1280]{1,0:T(8,128)S(1)}, f32[128,1280]{1,0:T(8,128)S(1)}, u32[]{:S(2)}, u32[]{:S(2)}) collective-permute-start(f32[128,1280]{1,0:T(8,128)S(1)} %get-tuple-element.88), channel_id=1, source_target_pairs={{0,32},{32,64},{64,96},{96,0},{1,33},{33,65},{65,97},{97,1},{2,34}... | collective-permute-start | bytes 1966088 | tf_op jit(solution)/shard_map/ppermute | solution.py:38
  75.7 19.6 %collective-permute-start.14 = (f32[128,1280]{1,0:T(8,128)S(1)}, f32[128,1280]{1,0:T(8,128)S(1)}, u32[]{:S(2)}, u32[]{:S(2)}) collective-permute-start(f32[128,1280]{1,0:T(8,128)S(1)} %get-tuple-element.94), channel_id=1, source_target_pairs={{0,96},{32,0},{64,32},{96,64},{1,97},{33,1},{65,33},{97,65},{2,98}... | collective-permute-start | bytes 1966088 | tf_op jit(solution)/shard_map/ppermute | solution.py:38
  82.8 41.6 %collective-permute-start.19 = (f32[4,128,768]{2,1,0:T(8,128)}, f32[4,128,768]{2,1,0:T(8,128)S(1)}, u32[]{:S(2)}, u32[]{:S(2)}) collective-permute-start(f32[4,128,768]{2,1,0:T(8,128)} %shard_map.94), channel_id=1, source_target_pairs={{0,16},{16,0},{1,17},{17,1},{2,18},{18,2},{3,19},{19,3},{4,20},{20... | collective-permute-start | bytes 4718600 | tf_op jit(solution)/shard_map/ppermute | solution.py:38
  92.0 31.0 %collective-permute-start.17 = (f32[2,512,256]{2,1,0:T(8,128)}, f32[2,512,256]{2,1,0:T(8,128)}, u32[]{:S(2)}, u32[]{:S(2)}) collective-permute-start(f32[2,512,256]{2,1,0:T(8,128)} %get-tuple-element.92), channel_id=1, source_target_pairs={{0,1},{1,2},{2,3},{3,0},{4,5},{5,6},{6,7},{7,4},{8,9},{9,10},{10,1... | collective-permute-start | bytes 3145736 | tf_op jit(solution)/shard_map/ppermute | solution.py:38
  92.2 30.8 %collective-permute-start.18 = (f32[2,512,256]{2,1,0:T(8,128)}, f32[2,512,256]{2,1,0:T(8,128)}, u32[]{:S(2)}, u32[]{:S(2)}) collective-permute-start(f32[2,512,256]{2,1,0:T(8,128)} %get-tuple-element.103), channel_id=1, source_target_pairs={{0,3},{1,0},{2,1},{3,2},{4,7},{5,4},{6,5},{7,6},{8,11},{9,8},{10,9... | collective-permute-start | bytes 3145736 | tf_op jit(solution)/shard_map/ppermute | solution.py:38
  102.6 30.6 %collective-permute-start.15 = (f32[2,128,1280]{2,1,0:T(8,128)}, f32[2,128,1280]{2,1,0:T(8,128)}, u32[]{:S(2)}, u32[]{:S(2)}) collective-permute-start(f32[2,128,1280]{2,1,0:T(8,128)} %get-tuple-element.95), channel_id=1, source_target_pairs={{0,32},{32,64},{64,96},{96,0},{1,33},{33,65},{65,97},{97,1},{2,34}... | collective-permute-start | bytes 3932168 | tf_op jit(solution)/shard_map/ppermute | solution.py:38
  102.6 30.6 %collective-permute-start.16 = (f32[2,128,1280]{2,1,0:T(8,128)}, f32[2,128,1280]{2,1,0:T(8,128)}, u32[]{:S(2)}, u32[]{:S(2)}) collective-permute-start(f32[2,128,1280]{2,1,0:T(8,128)} %get-tuple-element.100), channel_id=1, source_target_pairs={{0,96},{32,0},{64,32},{96,64},{1,97},{33,1},{65,33},{97,65},{2,98}... | collective-permute-start | bytes 3932168 | tf_op jit(solution)/shard_map/ppermute | solution.py:38
  128.4 40.3 %collective-permute-start.24 = (f32[512,256]{1,0:T(8,128)S(1)}, f32[512,256]{1,0:T(8,128)S(1)}, u32[]{:S(2)}, u32[]{:S(2)}) collective-permute-start(f32[512,256]{1,0:T(8,128)S(1)} %fusion.6), channel_id=1, source_target_pairs={{0,4},{4,0},{1,5},{5,1},{2,6},{6,2},{3,7},{7,3},{8,12},{12,8},{9,1... | collective-permute-start | bytes 1572872 | tf_op jit(solution)/shard_map/ppermute | solution.py:38
  134.6 51.9 %collective-permute-start.20 = (f32[128,1280]{1,0:T(8,128)S(1)}, f32[128,1280]{1,0:T(8,128)S(1)}, u32[]{:S(2)}, u32[]{:S(2)}) collective-permute-start(f32[128,1280]{1,0:T(8,128)S(1)} %fusion.1), channel_id=1, source_target_pairs={{0,16},{16,0},{1,17},{17,1},{2,18},{18,2},{3,19},{19,3},{4,20},{20... | collective-permute-start | bytes 1966088 | tf_op jit(solution)/shard_map/ppermute | solution.py:38
  139.3 14.7 %collective-permute-start.26 = (f32[1]{0:T(128)}, f32[1]{0:T(128)}, u32[]{:S(2)}, u32[]{:S(2)}) collective-permute-start(f32[1]{0:T(128)} %add.316), channel_id=1, source_target_pairs={{0,16},{16,0},{1,17},{17,1},{2,18},{18,2},{3,19},{19,3},{4,20},{20... | collective-permute-start | bytes 20 | tf_op jit(solution)/shard_map/ppermute | solution.py:44
  162.1 18.7 %collective-permute-start.21 = (f32[128,768]{1,0:T(8,128)S(1)}, f32[128,768]{1,0:T(8,128)S(1)}, u32[]{:S(2)}, u32[]{:S(2)}) collective-permute-start(f32[128,768]{1,0:T(8,128)S(1)} %get-tuple-element.111), channel_id=1, source_target_pairs={{0,32},{32,64},{64,96},{96,0},{1,33},{33,65},{65,97},{97,1},{2,34}... | collective-permute-start | bytes 1179656 | tf_op jit(solution)/shard_map/ppermute | solution.py:38
  164.1 16.7 %collective-permute-start.22 = (f32[128,768]{1,0:T(8,128)S(1)}, f32[128,768]{1,0:T(8,128)S(1)}, u32[]{:S(2)}, u32[]{:S(2)}) collective-permute-start(f32[128,768]{1,0:T(8,128)S(1)} %get-tuple-element.112), channel_id=1, source_target_pairs={{0,64},{32,96},{64,0},{96,32},{1,65},{33,97},{65,1},{97,33},{2,66}... | collective-permute-start | bytes 1179656 | tf_op jit(solution)/shard_map/ppermute | solution.py:38
  164.5 16.3 %collective-permute-start.23 = (f32[128,768]{1,0:T(8,128)S(1)}, f32[128,768]{1,0:T(8,128)S(1)}, u32[]{:S(2)}, u32[]{:S(2)}) collective-permute-start(f32[128,768]{1,0:T(8,128)S(1)} %get-tuple-element.113), channel_id=1, source_target_pairs={{0,96},{32,0},{64,32},{96,64},{1,97},{33,1},{65,33},{97,65},{2,98}... | collective-permute-start | bytes 1179656 | tf_op jit(solution)/shard_map/ppermute | solution.py:38
  (38 other events, 409.9 us)
